TPU v7x, 32 devices: a whole 2x2x4 slice. The times are simulated.
32 devices in a mesh: gx: 4 (over z), gy: 2 (over y), gz: 4 (over x, core).
Axes of the slice: x: 2, y: 2, z: 4, core: 2. Of those that a mesh axis runs over, the one named last changes fastest.
Arguments:
- positions: float32 [8, 4, 8, 3, 128], P('gx', 'gy', 'gz'), may hold values from 0 to 64, as said below
- velocities: float32 [8, 4, 8, 3, 128], P('gx', 'gy', 'gz'), may hold values from -5 to 5
- species: int32 [8, 4, 8, 128], P('gx', 'gy', 'gz'), may hold values from 0 to 3, as said below
- neighbour_blocks: int32 [8, 4, 8, 8], P('gx', 'gy', 'gz'), may hold values from 0 to 27, as said below
- embedding: bfloat16 [4, 64], replicated, may hold values from -6 to 6
- w_send: bfloat16 [2, 64, 64], replicated, may hold values from -0.75 to 0.75
- w_radial: float32 [2, 8, 64], replicated, may hold values from -4 to 4
- w_update: bfloat16 [2, 64, 64], replicated, may hold values from -0.75 to 0.75
- w_out: bfloat16 [64, 64], replicated, may hold values from -0.75 to 0.75
- w_energy: float32 [64], replicated, may hold values from -5 to 5
- masses: float32 [4], replicated, may hold values from 0.5 to 8
Outputs:
- displacement: float32 [8, 4, 8, 3, 128], P('gx', 'gy', 'gz')
- new_velocity: float32 [8, 4, 8, 3, 128], P('gx', 'gy', 'gz')
Inputs may be any that keep to these rules, and one draw needn't show every extreme that they name: `positions`: each atom slot lies in the cube of side 8 whose lowest corner is 8 times its block's coordinates. `species`: 0 marks an empty slot; in each block the empty slots follow the occupied ones, and at least 32 slots are occupied. `neighbour_blocks`: entry o below 27 is the offset 9 (dx + 1) + 3 (dy + 1) + (dz + 1) of a source block; 27 marks an empty slot. The first entry is 13, the block itself; live entries of a block are distinct and come before its empty slots; each block has two or more live entries.
All inputs are finite; a program needn't handle non-finite values.
Results may differ from a plain program's by a relative error of at most 0.039.
Values may be sent and summed in bfloat16 or wider, within the bound.
A program may use at most 64 MiB of HBM per device.

v0:
```python
import jax
import jax.numpy as jnp
from jax import lax
from jax.sharding import PartitionSpec as P

soft_sq = 0.25
cut_sq = 25.0
gamma_width = 2.56
time_step = 1.0
target_slot = 0.25
tiny_eps = 1e-06


def padded(cells, sides, width):
    for axis, dim in sides:
        count = lax.axis_size(axis)
        ends = count - 1
        head = lax.slice_in_dim(cells, 0, width, axis=dim)
        tail = lax.slice_in_dim(cells, cells.shape[dim] - width, cells.shape[dim], axis=dim)
        cells = jnp.concatenate(
            [
                lax.ppermute(tail, axis, [(i, (i + 1) % count) for i in range(ends)]),
                cells,
                lax.ppermute(head, axis, [((i + 1) % count, i) for i in range(ends)]),
            ],
            axis=dim,
        )
    return cells


def slot_tables(neighbour_blocks):
    size_x, size_y, size_z, slot_count = neighbour_blocks.shape
    is_live = neighbour_blocks < 27
    offset = jnp.where(is_live, neighbour_blocks, 13)
    step_x = offset // 9 - 1
    step_y = offset // 3 % 3 - 1
    step_z = offset % 3 - 1
    index_x = lax.broadcasted_iota(jnp.int32, neighbour_blocks.shape, 0)
    index_y = lax.broadcasted_iota(jnp.int32, neighbour_blocks.shape, 1)
    index_z = lax.broadcasted_iota(jnp.int32, neighbour_blocks.shape, 2)
    source = ((index_x + 1 + step_x) * (size_y + 2) + (index_y + 1 + step_y)) * (size_z + 2) + (
        index_z + 1 + step_z
    )
    target = (
        ((index_x[..., 0] + 1) * (size_y + 2) + index_y[..., 0] + 1) * (size_z + 2)
        + index_z[..., 0]
        + 1
    )
    return (
        source.reshape(-1, slot_count),
        target.reshape(-1),
        is_live.astype(jnp.float32).reshape(-1, slot_count),
        (neighbour_blocks == 13).astype(jnp.float32).reshape(-1, slot_count),
    )


def feature_table(species_ext, embedding):
    kind_count = embedding.shape[0]
    onehot = (
        species_ext[..., None, :] == lax.broadcasted_iota(jnp.int32, (kind_count, 1), 0)
    ).astype(jnp.float32)
    return jnp.einsum(
        "sc,...sa->...ca", embedding.astype(jnp.float32), onehot, precision=lax.Precision.HIGHEST
    )


def inverse_mass(species, masses):
    kind_count = masses.shape[0]
    onehot = (species[..., None, :] == lax.broadcasted_iota(jnp.int32, (kind_count, 1), 0)).astype(
        jnp.float32
    )
    return (
        1.0
        / jnp.einsum("s,...sa->...a", masses, onehot, precision=lax.Precision.HIGHEST)[..., None, :]
    )


def pair_kernel(
    target_pos, target_real, source_pos, source_real, slot_live, slot_self, basis_count
):
    offset = source_pos[:, :, None, :] - target_pos[None, :, :, None]
    squared = jnp.sum(offset * offset, axis=1)
    distance = jnp.sqrt(squared + soft_sq)
    cutoff = jnp.square(jax.nn.relu(1.0 - squared / cut_sq))
    atom_count = target_pos.shape[-1]
    diagonal = (
        lax.broadcasted_iota(jnp.int32, (atom_count, atom_count), 0)
        == lax.broadcasted_iota(jnp.int32, (atom_count, atom_count), 1)
    ).astype(jnp.float32)
    weight = (
        cutoff * target_real[None, :, None] * source_real[:, None, :] * slot_live[:, None, None]
    )
    weight = weight * (1.0 - slot_self[:, None, None] * diagonal[None])
    centers = (lax.iota(jnp.float32, basis_count) + 0.5) * (5.0 / basis_count)
    radial = jnp.exp(-gamma_width * jnp.square(distance[None] - centers[:, None, None, None]))
    return (weight[None] * radial).astype(jnp.bfloat16)


def block_message(kernel, source_feat, w_send, w_radial):
    sender = jnp.einsum(
        "qcj,cd->qdj", source_feat.astype(jnp.bfloat16), w_send, preferred_element_type=jnp.float32
    ).astype(jnp.bfloat16)
    partial_value = jnp.einsum("kqij,qdj->kdi", kernel, sender, preferred_element_type=jnp.float32)
    return jnp.sum(partial_value * w_radial[:, :, None], axis=0).astype(jnp.bfloat16)


def block_update(target_feat, message, w_update):
    update = jnp.einsum("ci,cd->di", message, w_update, preferred_element_type=jnp.float32)
    return target_feat + jax.nn.silu(update)


def layer_one(flat_pos, flat_feat, flat_real, tables, w_send, w_radial, w_update):

    def one_block(entry):
        source_idx, target_idx, slot_live, slot_self = entry
        kernel = pair_kernel(
            flat_pos[target_idx],
            flat_real[target_idx],
            jnp.take(flat_pos, source_idx, axis=0),
            jnp.take(flat_real, source_idx, axis=0),
            slot_live,
            slot_self,
            w_radial.shape[1],
        )
        message = block_message(
            kernel, jnp.take(flat_feat, source_idx, axis=0), w_send[0], w_radial[0]
        )
        return block_update(flat_feat[target_idx], message, w_update[0])

    layer_out = lax.map(jax.checkpoint(one_block), tables)
    return lax.optimization_barrier(layer_out.astype(jnp.bfloat16)).astype(jnp.float32)


def layer_two_energy(
    flat_pos, flat_feat, flat_real, tables, w_send, w_radial, w_update, w_out, w_energy
):

    def one_block(entry):
        source_idx, target_idx, slot_live, slot_self = entry
        target_real = flat_real[target_idx]
        kernel = pair_kernel(
            flat_pos[target_idx],
            target_real,
            jnp.take(flat_pos, source_idx, axis=0),
            jnp.take(flat_real, source_idx, axis=0),
            slot_live,
            slot_self,
            w_radial.shape[1],
        )
        message = block_message(
            kernel, jnp.take(flat_feat, source_idx, axis=0), w_send[1], w_radial[1]
        )
        second = block_update(flat_feat[target_idx], message, w_update[1])
        hidden = jnp.einsum(
            "ci,cd->di", second.astype(jnp.bfloat16), w_out, preferred_element_type=jnp.float32
        )
        per_atom = jnp.sum(jax.nn.silu(hidden) * w_energy[:, None], axis=0) * target_real
        return jnp.sum(per_atom)

    return jnp.sum(lax.map(jax.checkpoint(one_block), tables))


def fold_along(grid, along, move):
    inner_len = grid.shape[along] - 2
    low_rim = lax.slice_in_dim(grid, 0, 1, axis=along)
    high_rim = lax.slice_in_dim(grid, inner_len + 1, inner_len + 2, axis=along)
    filler_shape = list(grid.shape)
    filler_shape[along] = inner_len - 2
    filler = jnp.zeros(filler_shape, grid.dtype)
    packed = jnp.concatenate([low_rim, filler, high_rim], axis=along)
    received = move(packed)
    returned = jnp.concatenate(
        [
            lax.slice_in_dim(received, 0, 1, axis=along),
            filler,
            lax.slice_in_dim(received, inner_len + 1, inner_len + 2, axis=along),
        ],
        axis=along,
    )
    return lax.slice_in_dim(grid, 1, inner_len + 1, axis=along) + returned


def send_first(packed):
    return padded(packed.astype(jnp.bfloat16), (("gx", 0),), 1).astype(packed.dtype)


def send_second(packed):
    return padded(packed.astype(jnp.bfloat16), (("gy", 1),), 1).astype(packed.dtype)


def send_third(packed):
    return padded(packed.astype(jnp.bfloat16), (("gz", 2),), 1).astype(packed.dtype)


def fold_grid(grid):
    grid = fold_along(grid, 2, send_third)
    grid = fold_along(grid, 1, send_second)
    return fold_along(grid, 0, send_first)


def local(
    positions,
    velocities,
    species,
    neighbour_blocks,
    embedding,
    w_send,
    w_radial,
    w_update,
    w_out,
    w_energy,
    masses,
):
    grid_x, grid_y, grid_z = (positions.shape[0], positions.shape[1], positions.shape[2])
    atom_count = positions.shape[-1]
    channels = w_send.shape[-1]
    ext_shape = (grid_x + 2, grid_y + 2, grid_z + 2)
    species_ext = padded(species, (("gx", 0), ("gy", 1), ("gz", 2)), 1)
    flat_feat = feature_table(species_ext, embedding).reshape(-1, channels, atom_count)
    flat_real = (species_ext > 0).astype(jnp.float32).reshape(-1, atom_count)
    tables = slot_tables(neighbour_blocks)
    inverse = inverse_mass(species, masses)

    def first_of(flat_pos):
        return layer_one(flat_pos, flat_feat, flat_real, tables, w_send, w_radial, w_update)

    def second_of(flat_pos, flat_hidden):
        return layer_two_energy(
            flat_pos, flat_hidden, flat_real, tables, w_send, w_radial, w_update, w_out, w_energy
        )

    def forces(coords):
        ghost_pos = padded(coords, (("gx", 0), ("gy", 1), ("gz", 2)), 1)
        flat_pos = ghost_pos.reshape(-1, 3, atom_count)
        layer_out, pull_one = jax.vjp(first_of, flat_pos)
        grid_feat = layer_out.reshape(grid_x, grid_y, grid_z, channels, atom_count).astype(
            jnp.bfloat16
        )
        ghost_feat = padded(grid_feat, (("gx", 0), ("gy", 1), ("gz", 2)), 1)
        flat_hidden = ghost_feat.astype(jnp.float32).reshape(-1, channels, atom_count)
        energy, pull_two = jax.vjp(second_of, flat_pos, flat_hidden)
        grad_pos, grad_feat = pull_two(jnp.ones((), jnp.float32))
        grad_pos = grad_pos.reshape(ext_shape + (3, atom_count))
        grad_feat = grad_feat.reshape(ext_shape + (channels, atom_count))
        folded = fold_grid(grad_feat)
        (grad_first,) = pull_one(folded.reshape(-1, channels, atom_count))
        total = fold_grid(grad_pos + grad_first.reshape(ext_shape + (3, atom_count)))
        return -total

    coords = positions
    velocity = velocities
    force_now = forces(coords)
    half_kick = velocity + 0.5 * time_step * force_now * inverse
    coords = coords + time_step * half_kick
    travelled = time_step * half_kick
    force_now = forces(coords)
    velocity = half_kick + 0.5 * time_step * force_now * inverse
    real_here = (species > 0).astype(jnp.float32)[..., None, :]
    local_kinetic = jnp.sum(real_here * 0.5 / inverse * velocity * velocity)
    kinetic = lax.psum(local_kinetic, ("gx", "gy", "gz"))
    slot_total = (
        positions.size // 3 * lax.axis_size("gx") * lax.axis_size("gy") * lax.axis_size("gz")
    )
    factor = jnp.sqrt(target_slot * slot_total / (kinetic + tiny_eps))
    return (travelled, velocity * factor)


def solution(mesh):
    placed = (
        P("gx", "gy", "gz", None, None),
        P("gx", "gy", "gz", None, None),
        P("gx", "gy", "gz", None),
        P("gx", "gy", "gz", None),
        P(),
        P(),
        P(),
        P(),
        P(),
        P(),
        P(),
    )
    return jax.shard_map(
        local,
        mesh=mesh,
        in_specs=placed,
        out_specs=(P("gx", "gy", "gz", None, None), P("gx", "gy", "gz", None, None)),
        check_vma=False,
    )
```

profile of v0, /device:TPU:0, one launch (start us, length us, event | category | flops | bytes accessed | tf_op | source)
XLA Modules:
  0.0 1163.7 jit_solution(16900740234506184976)
XLA Ops:
  1.4 4.9 collective-permute-start
  8.3 4.5 collective-permute-start.6
  22.3 4.5 collective-permute-start.2
  34.6 4.5 collective-permute-start.8
  46.5 97.3 %while.86 = (s32[]{:T(128)}, bf16[8,64,128]{2,1,0:T(8,128)(2,1)S(1)}, s32[8]{0:T(128)}, f32[64,64,128]{2,1,0:T(8,128)S(1)}, s32[8,8]{1,0:T(8,128)}, /*index=5*/b...) while((s32[]{:T(128)}, ...), condition=%wide.region_3.7_spmd.clone, body=%wide.region_0.6_spmd.clone.sunk | while | flops 151721024 | bytes 3953395 | solution.py:130
  145.8 5.2 collective-permute-start.12
  154.5 4.6 collective-permute-start.14
  164.2 4.0 collective-permute-start.16
  171.3 183.5 %while.88 = (s32[]{:T(128)}, f32[64,3,128]{2,1,0:T(4,128)S(1)}, f32[64,64,128]{2,1,0:T(8,128)}, s32[8,8]{1,0:T(8,128)}, s32[8]{0:T(128)}, /*index=5*/f32[8,8]{1,...) while((s32[]{:T(128)}, f32[64,3,128]{2,1,0:T(4,128)S(1)}, ...), condition=%wide.region_13.20_spmd.clone, body=%wide.region_4.19_spmd.clone.sunk | while | flops 456455776 | bytes 20435976 | solution.py:160
  358.1 6.8 collective-permute-start.18
  368.4 5.8 collective-permute-start.20
  378.5 5.4 collective-permute-start.22
  386.1 186.1 %while.89 = (s32[]{:T(128)}, f32[64,3,128]{2,1,0:T(4,128)S(1)}, s32[8,8]{1,0:T(8,128)}, s32[8]{0:T(128)}, f32[8,8]{1,0:T(8,128)}, /*index=5*/f32[8,8]{1,0:T(8,12...) while((s32[]{:T(128)}, f32[64,3,128]{2,1,0:T(4,128)S(1)}, ...), condition=%wide.region_22.30_spmd.clone, body=%wide.region_14.29_spmd.clone.sunk | while | flops 304977376 | bytes 10501989 | solution.py:130
  574.5 5.8 collective-permute-start.24
  582.8 4.5 collective-permute-start.26
  590.0 4.5 collective-permute-start.28
  598.5 4.8 collective-permute-start.30
  606.0 4.5 collective-permute-start.32
  613.3 3.6 collective-permute-start.34
  618.6 100.6 %while.87 = (s32[]{:T(128)}, bf16[8,64,128]{2,1,0:T(8,128)(2,1)S(1)}, s32[8]{0:T(128)}, f32[64,64,128]{2,1,0:T(8,128)S(1)}, s32[8,8]{1,0:T(8,128)}, /*index=5*/b...) while((s32[]{:T(128)}, ...), condition=%wide.region_26.34_spmd.clone, body=%wide.region_23.33_spmd.clone.sunk | while | flops 151721024 | bytes 3961771 | solution.py:130
  720.5 4.5 collective-permute-start.36
  728.3 4.6 collective-permute-start.38
  736.7 6.7 collective-permute-start.40
  746.3 185.6 %while.90 = (s32[]{:T(128)}, f32[64,3,128]{2,1,0:T(4,128)S(1)}, f32[64,64,128]{2,1,0:T(8,128)}, s32[8,8]{1,0:T(8,128)}, s32[8]{0:T(128)}, /*index=5*/f32[8,8]{1,...) while((s32[]{:T(128)}, f32[64,3,128]{2,1,0:T(4,128)S(1)}, ...), condition=%wide.region_36.44_spmd.clone, body=%wide.region_27.43_spmd.clone.sunk | while | flops 456455776 | bytes 20435976 | solution.py:160
  935.1 9.0 collective-permute-start.42
  946.9 4.6 collective-permute-start.44
  955.5 5.1 collective-permute-start.46
  962.4 128.7 %while.91 = (s32[]{:T(128)}, f32[64,3,128]{2,1,0:T(4,128)S(1)}, s32[8,8]{1,0:T(8,128)}, s32[8]{0:T(128)}, f32[8,8]{1,0:T(8,128)}, /*index=5*/f32[8,8]{1,0:T(8,12...) while((s32[]{:T(128)}, f32[64,3,128]{2,1,0:T(4,128)S(1)}, ...), condition=%wide.region_45.53_spmd.clone, body=%wide.region_37.52_spmd.clone.sunk | while | flops 304977376 | bytes 9649093 | solution.py:130
  1092.5 5.3 collective-permute-start.48
  1100.2 4.5 collective-permute-start.50
  1107.4 4.6 collective-permute-start.52
  1114.0 48.1 %psum.7 = f32[]{:T(128)} all-reduce(f32[]{:T(128)} %get-tuple-element.1991), channel_id=1, replica_groups=mesh['gx'=4,'gy'=2,'gz'=4] {'gx','gy','gz'}, use_global_device_ids=true, to_apply=%region_47.55 | all-reduce | flops 1 | bytes 8 | tf_op jit(solution)/shard_map/psum | solution.py:260
  (1905 shorter events, 885.0 us)
Async XLA Ops:
  1.4 18.9 %collective-permute-start = (s32[1,2,2,128]{3,2,1,0:T(2,128)S(1)}, s32[1,2,2,128]{3,2,1,0:T(2,128)S(1)}, u32[]{:S(2)}, u32[]{:S(2)}) collective-permute-start(s32[1,2,2,128]{3,2,1,0:T(2,128)S(1)} %get-tuple-element.2126), channel_id=1, source_target_pairs={{0,8},{8,16},{16,24},{1,9},{9,17},{17,25},{2,10},{10,18},{18,26},{... | collective-permute-start | bytes 6152 | tf_op jit(solution)/shard_map/ppermute | solution.py:22
  6.3 14.7 %collective-permute-start.1 = (s32[1,2,2,128]{3,2,1,0:T(2,128)S(1)}, s32[1,2,2,128]{3,2,1,0:T(2,128)S(1)}, u32[]{:S(2)}, u32[]{:S(2)}) collective-permute-start(s32[1,2,2,128]{3,2,1,0:T(2,128)S(1)} %get-tuple-element.2125), channel_id=1, source_target_pairs={{8,0},{16,8},{24,16},{9,1},{17,9},{25,17},{10,2},{18,10},{26,18},{... | collective-permute-start | bytes 6152 | tf_op jit(solution)/shard_map/ppermute | solution.py:24
  8.3 24.2 %collective-permute-start.6 = (f32[1,2,2,3,128]{4,2,3,1,0:T(2,128)S(1)}, f32[1,2,2,3,128]{4,2,3,1,0:T(2,128)S(1)}, u32[]{:S(2)}, u32[]{:S(2)}) collective-permute-start(f32[1,2,2,3,128]{4,2,3,1,0:T(2,128)S(1)} %get-tuple-element.2120), channel_id=1, source_target_pairs={{0,8},{8,16},{16,24},{1,9},{9,17},{17,25},{2,10},{10,18},{18,26},{... | collective-permute-start | bytes 18440 | tf_op jit(solution)/shard_map/ppermute | solution.py:22
  12.9 20.4 %collective-permute-start.7 = (f32[1,2,2,3,128]{4,2,3,1,0:T(2,128)S(1)}, f32[1,2,2,3,128]{4,2,3,1,0:T(2,128)S(1)}, u32[]{:S(2)}, u32[]{:S(2)}) collective-permute-start(f32[1,2,2,3,128]{4,2,3,1,0:T(2,128)S(1)} %get-tuple-element.2119), channel_id=1, source_target_pairs={{8,0},{16,8},{24,16},{9,1},{17,9},{25,17},{10,2},{18,10},{26,18},{... | collective-permute-start | bytes 18440 | tf_op jit(solution)/shard_map/ppermute | solution.py:24
  21.0 6.5 collective-permute-start.3
  28.2 11.0 collective-permute-start.5
  29.5 9.7 collective-permute-start.4
  144.5 6.9 collective-permute-start.13
  145.8 7.3 collective-permute-start.12
  153.2 7.8 collective-permute-start.15
  154.5 7.6 collective-permute-start.14
  356.7 8.3 collective-permute-start.19
  358.1 8.0 collective-permute-start.18
  367.1 7.2 collective-permute-start.21
  368.4 7.7 collective-permute-start.20
  377.2 7.9 collective-permute-start.23
  378.5 6.8 collective-permute-start.22
  573.2 7.1 collective-permute-start.25
  574.5 6.7 collective-permute-start.24
  581.5 6.7 collective-permute-start.27
  588.7 7.1 collective-permute-start.29
  727.0 6.9 collective-permute-start.39
  728.3 7.1 collective-permute-start.38
  735.4 8.1 collective-permute-start.41
  736.7 7.7 collective-permute-start.40
  933.7 10.4 collective-permute-start.43
  935.1 10.1 collective-permute-start.42
  945.6 6.9 collective-permute-start.45
  946.9 7.1 collective-permute-start.44
  955.5 6.8 collective-permute-start.46
  1091.2 6.6 collective-permute-start.49
  1106.1 6.5 collective-permute-start.53
  (232 other events, 1338.6 us)
where the time goes:
time: 1180 us; the launch traced here: 1160 us
  local copies, waits for them, and re-layouts  362 us (31%)
  matrix products  233 us (20%)
  other arithmetic  219 us (19%)
  starting transfers between devices  168 us (14%)
  loops' own time  101 us (9%)
  blocking collectives  48.1 us (4%)
  waiting for transfers between devices  29.1 us (2%)
    dot_general x80, matrix products, block_message(): jnp.einsum('kqij,qdj->kdi', kernel, sender, preferred_element_type=jnp.fl...  168 us
    ppermute x27, starting transfers between devices, padded(): lax.ppermute(tail, axis, [(i, (i + 1) % count) for i in range(ends)])  133 us
    gather x48, local copies, waits for them, and re-layouts, one_block(): jnp.take(flat_feat, source_idx, axis=0)  73.3 us
    gather x48, local copies, waits for them, and re-layouts, one_block(): jnp.take(flat_pos, source_idx, axis=0)  70.9 us
    another operation x4, loops' own time, layer_one(): layer_out = lax.map(jax.checkpoint(one_block), tables)  67.8 us
    dynamic_slice x48, local copies, waits for them, and re-layouts, layer_one(): layer_out = lax.map(jax.checkpoint(one_block), tables)  62.7 us
    squeeze x80, local copies, waits for them, and re-layouts, layer_one(): layer_out = lax.map(jax.checkpoint(one_block), tables)  55.2 us
    add_any x32, other arithmetic, layer_two_energy(): return jnp.sum(lax.map(jax.checkpoint(one_block), tables))  54.2 us
  transfers between devices with their start and end apart: 54, of which 29 were waited for; matrix products, arithmetic and copies ran while one was open for 1% of the time, Pallas kernels for 0%

commit v1 on v0

v1 whole, which is shorter than its diff:
```python
import functools
import math

import jax
import jax.numpy as jnp
from jax import lax
from jax.experimental import pallas as pl
from jax.experimental.pallas import tpu as pltpu
from jax.sharding import PartitionSpec as P

soft_sq = 0.25
cut_sq = 25.0
gamma_width = 2.56
time_step = 1.0
target_slot = 0.25
tiny_eps = 1e-06
LOG2E = math.log2(math.e)
CHUNK = 32
bf16 = jnp.bfloat16
f32 = jnp.float32

SIDES = (("gx", 0), ("gy", 1), ("gz", 2))


def padded(cells):
    for axis, dim in SIDES:
        count = lax.axis_size(axis)
        ends = count - 1
        head = lax.slice_in_dim(cells, 0, 1, axis=dim)
        tail = lax.slice_in_dim(cells, cells.shape[dim] - 1, cells.shape[dim], axis=dim)
        cells = jnp.concatenate(
            [
                lax.ppermute(tail, axis, [(i, i + 1) for i in range(ends)]),
                cells,
                lax.ppermute(head, axis, [(i + 1, i) for i in range(ends)]),
            ],
            axis=dim,
        )
    return cells


def folded(grid):
    for axis, dim in reversed(SIDES):
        count = lax.axis_size(axis)
        ends = count - 1
        size = grid.shape[dim]
        low = lax.slice_in_dim(grid, 0, 1, axis=dim)
        high = lax.slice_in_dim(grid, size - 1, size, axis=dim)
        from_low = lax.ppermute(high, axis, [(i, i + 1) for i in range(ends)])
        from_high = lax.ppermute(low, axis, [(i + 1, i) for i in range(ends)])
        inner = lax.slice_in_dim(grid, 1, size - 1, axis=dim)
        first = lax.slice_in_dim(inner, 0, 1, axis=dim) + from_low
        last = lax.slice_in_dim(inner, size - 3, size - 2, axis=dim)
        if size == 3:
            grid = first + from_high
        else:
            middle = lax.slice_in_dim(inner, 1, size - 3, axis=dim)
            grid = jnp.concatenate([first, middle, last + from_high], axis=dim)
    return grid


def slot_tables(neighbour_blocks):
    size_x, size_y, size_z, slot_count = neighbour_blocks.shape
    is_live = neighbour_blocks < 27
    offset = jnp.where(is_live, neighbour_blocks, 13)
    index_x = lax.broadcasted_iota(jnp.int32, neighbour_blocks.shape, 0)
    index_y = lax.broadcasted_iota(jnp.int32, neighbour_blocks.shape, 1)
    index_z = lax.broadcasted_iota(jnp.int32, neighbour_blocks.shape, 2)
    source = (
        (index_x + offset // 9) * (size_y + 2) + (index_y + offset // 3 % 3)
    ) * (size_z + 2) + (index_z + offset % 3)
    live = jnp.sum(is_live.astype(jnp.int32), axis=-1)
    return source.reshape(-1, slot_count), live.reshape(-1)


def basis_constants(basis_count):
    step = 5.0 / basis_count
    mid = basis_count // 2
    centers = [(k + 0.5) * step for k in range(basis_count)]
    scales = [math.exp(-gamma_width * (centers[k] - centers[mid]) ** 2) for k in range(basis_count)]
    return step, mid, centers, scales


def geometry(own, cols, row0, is_self, basis_count):
    step, mid, centers, _ = basis_constants(basis_count)
    rows = slice(row0, row0 + CHUNK)
    dx = cols[rows, 0:1] - own[0:1, :]
    dy = cols[rows, 1:2] - own[1:2, :]
    dz = cols[rows, 2:3] - own[2:3, :]
    squared = jnp.minimum(dx * dx + dy * dy + dz * dz, cut_sq)
    shape = squared.shape
    j_index = lax.broadcasted_iota(jnp.int32, shape, 0) + row0
    i_index = lax.broadcasted_iota(jnp.int32, shape, 1)
    cut = (cut_sq - squared) * (1.0 / cut_sq)
    cut = jnp.where((j_index == i_index) & is_self, 0.0, cut)
    soft = squared + soft_sq
    inv = lax.rsqrt(soft)
    shift = soft * inv - centers[mid]
    bell = jnp.exp2((-gamma_width * LOG2E) * (shift * shift))
    slope = shift * (2.0 * gamma_width * step * LOG2E)
    return cut, inv, bell, jnp.exp2(slope), jnp.exp2(-slope)


def radial_powers(start, up, down, basis_count):
    mid = basis_count // 2
    powers = [None] * basis_count
    powers[mid] = start
    for k in range(mid + 1, basis_count):
        powers[k] = powers[k - 1] * up
    for k in range(mid - 1, -1, -1):
        powers[k] = powers[k + 1] * down
    return powers


def fill_kernel(store, own, cols, is_self, basis_count):
    atoms = own.shape[-1]
    for row0 in range(0, atoms, CHUNK):
        cut, _, bell, up, down = geometry(own, cols, row0, is_self, basis_count)
        for k, value in enumerate(radial_powers(cut * cut * bell, up, down, basis_count)):
            store[k, row0 : row0 + CHUNK, :] = value.astype(bf16)


def pick(species_row, table, first):
    out = None
    for s in range(first, table.shape[0]):
        hit = species_row == float(s)
        out = jnp.where(hit, table[s], 0.0 if out is None else out)
    return out


def widened(radial, value):
    return jnp.concatenate(
        [(radial[k] * value).astype(bf16) for k in range(radial.shape[0])], axis=1
    )


def silu_grad(value):
    gate = jax.nn.sigmoid(value)
    return gate * (1.0 + value * (1.0 - gate))


def dot(a, b):
    return jnp.dot(a, b, preferred_element_type=f32)


def first_kernel(target_of, src, live, pos, send_tab, feat_tab, radial, update_t, send_t,
                 h1_out, u1_out, s2_out, store):
    basis_count = radial.shape[0]
    channels, atoms = send_tab.shape[1:]
    for b, home in enumerate(target_of):
        own = pos[home]

        def slot(q, total):
            block = pos[src[b, q]]
            fill_kernel(store, own, block.T, q == 0, basis_count)
            wide = widened(radial, pick(block[3:4, :], send_tab, 1))
            return total + dot(wide, store[...].reshape(basis_count * atoms, atoms))

        total = lax.fori_loop(0, live[b], slot, jnp.zeros((channels, atoms), f32))
        update = dot(update_t[...], total.astype(bf16))
        species = own[3:4, :]
        hidden = (pick(species, feat_tab, 0) + update * jax.nn.sigmoid(update)).astype(bf16)
        h1_out[b] = hidden
        u1_out[b] = update
        s2_out[b] = jnp.where(species > 0.0, dot(send_t[...], hidden), 0.0).astype(bf16)


def second_kernel(target_of, src, live, pos, s2, h1, radial, update, update_t, out, out_t, energy,
                  g2_out, dh2_out, ds_out, store, acc):
    basis_count = radial.shape[0]
    channels, atoms = s2.shape[1:]
    acc[...] = jnp.zeros_like(acc)
    for b, home in enumerate(target_of):
        own = pos[home]

        def gather(q, total):
            where = src[b, q]
            fill_kernel(store.at[q], own, pos[where].T, q == 0, basis_count)
            wide = widened(radial, s2[where].astype(f32))
            return total + dot(wide, store[q].reshape(basis_count * atoms, atoms))

        total = lax.fori_loop(0, live[b], gather, jnp.zeros((channels, atoms), f32))
        up = dot(update_t[...], total.astype(bf16))
        second = h1[b].astype(f32) + up * jax.nn.sigmoid(up)
        hidden = dot(out_t[...], second.astype(bf16))
        real = own[3:4, :] > 0.0
        d_hidden = jnp.where(real, energy[...] * silu_grad(hidden), 0.0)
        d_second = dot(out[...], d_hidden.astype(bf16))
        dh2_out[b] = d_second
        g2 = dot(update[...], (d_second * silu_grad(up)).astype(bf16)).astype(bf16)
        g2_out[b] = g2
        wide = widened(radial, g2.astype(f32))

        def scatter(q, carry):
            flat = jnp.concatenate([store[q, k] for k in range(basis_count)], axis=1)
            where = src[b, q]
            acc[where] += lax.dot_general(
                wide, flat, (((1,), (1,)), ((), ())), preferred_element_type=f32
            )
            return carry

        lax.fori_loop(0, live[b], scatter, 0)
    ds_out[...] = acc[...].astype(bf16)


def split_rows(rel):
    row = lax.broadcasted_iota(jnp.int32, rel.shape, 0)
    rel = jnp.where(row < 3, rel, jnp.where(row == 3, 1.0, 0.0))
    high = rel.astype(bf16)
    low = (rel - high.astype(f32)).astype(bf16)
    return rel, jnp.concatenate([high, low], axis=0)


def third_kernel(target_of, src, live, pos, s2, g2, dh2, ds, u1, send_tab, radial_one, radial_two,
                 send, update, grad_out, wide, parts):
    basis_count = radial_one.shape[0]
    atoms = pos.shape[-1]
    _, _, centers, _ = basis_constants(basis_count)
    grad_out[...] = jnp.zeros_like(grad_out)
    for b, home in enumerate(target_of):
        own = pos[home]
        real = own[3:4, :] > 0.0
        dh1 = dh2[b] + dot(send[...], ds[b])
        du1 = dh1 * silu_grad(u1[b])
        g1 = jnp.where(real, dot(update[...], du1.astype(bf16)), 0.0).astype(bf16)
        wide[...] = jnp.concatenate(
            [widened(radial_one, g1.astype(f32)), widened(radial_two, g2[b].astype(f32))], axis=0
        )
        origin = own[:, 0:1]
        own_rel, own_split = split_rows(own - origin)

        def slot(q, total):
            where = src[b, q]
            block = pos[where]
            cols = block.T
            sender = jnp.concatenate(
                [pick(block[3:4, :], send_tab, 1), s2[where].astype(f32)], axis=0
            )
            parts[...] = dot(sender.T.astype(bf16), wide[...])
            pieces = []
            for row0 in range(0, atoms, CHUNK):
                cut, inv, bell, up, down = geometry(own, cols, row0, q == 0, basis_count)
                plain = jnp.zeros_like(cut)
                moment = jnp.zeros_like(cut)
                for k, value in enumerate(radial_powers(bell, up, down, basis_count)):
                    term = value * parts[row0 : row0 + CHUNK, k * atoms : (k + 1) * atoms]
                    plain = plain + term
                    moment = moment + centers[k] * term
                scaled = gamma_width * cut
                pieces.append(
                    (cut * (moment * (scaled * inv) - plain * (scaled + 2.0 / cut_sq))).astype(bf16)
                )
            slope = jnp.concatenate(pieces, axis=0)
            block_rel, block_split = split_rows(block - origin)
            at_target = dot(block_split, slope)
            at_source = lax.dot_general(
                own_split, slope, (((1,), (1,)), ((), ())), preferred_element_type=f32
            )
            at_target = at_target[:8] + at_target[8:]
            at_source = at_source[:8] + at_source[8:]
            grad_out[where] += 2.0 * (block_rel * at_source[3:4, :] - at_source)
            return total + 2.0 * (own_rel * at_target[3:4, :] - at_target)

        total = lax.fori_loop(0, live[b], slot, jnp.zeros_like(own))
        grad_out[home] += total


def call(kernel, outs, scratch, smem, args):
    return pl.pallas_call(
        kernel,
        out_shape=outs,
        in_specs=[pl.BlockSpec(memory_space=pltpu.SMEM)] * len(smem)
        + [pl.BlockSpec(memory_space=pltpu.VMEM)] * len(args),
        out_specs=[pl.BlockSpec(memory_space=pltpu.VMEM)] * len(outs),
        scratch_shapes=scratch,
        compiler_params=pltpu.CompilerParams(vmem_limit_bytes=48 << 20),
    )(*smem, *args)


def local(
    positions,
    velocities,
    species,
    neighbour_blocks,
    embedding,
    w_send,
    w_radial,
    w_update,
    w_out,
    w_energy,
    masses,
):
    grid_x, grid_y, grid_z = positions.shape[:3]
    atoms = positions.shape[-1]
    channels = w_send.shape[-1]
    basis_count = w_radial.shape[1]
    kinds = masses.shape[0]
    blocks = grid_x * grid_y * grid_z
    ext_shape = (grid_x + 2, grid_y + 2, grid_z + 2)
    ext_count = ext_shape[0] * ext_shape[1] * ext_shape[2]
    target_of = [
        ((x + 1) * ext_shape[1] + y + 1) * ext_shape[2] + z + 1
        for x in range(grid_x)
        for y in range(grid_y)
        for z in range(grid_z)
    ]
    src, live = slot_tables(neighbour_blocks)
    smem = (src, live)
    scales = jnp.array(basis_constants(basis_count)[3], f32)
    radial = jnp.broadcast_to(
        (w_radial * scales[None, :, None])[..., None], (2, basis_count, channels, atoms)
    )
    send_rows = jnp.dot(embedding, w_send[0], preferred_element_type=f32).astype(bf16).astype(f32)
    send_tab = jnp.broadcast_to(send_rows[..., None], (kinds, channels, atoms))
    feat_tab = jnp.broadcast_to(embedding.astype(f32)[..., None], (kinds, channels, atoms))
    energy = jnp.broadcast_to(w_energy[:, None], (channels, atoms))
    update_t = jnp.swapaxes(w_update, 1, 2)
    species_row = species.astype(f32)[..., None, :]
    filler = jnp.zeros((grid_x, grid_y, grid_z, 4, atoms), f32)

    def shaped(count, dtype):
        return jax.ShapeDtypeStruct((count, channels, atoms), dtype)

    def grid_of(value):
        return value.reshape((grid_x, grid_y, grid_z) + value.shape[1:])

    def flat(value):
        return value.reshape((-1,) + value.shape[3:])

    def forces(coords):
        pos = flat(padded(jnp.concatenate([coords, species_row, filler], axis=3)))
        h1, u1, s2_own = call(
            functools.partial(first_kernel, target_of),
            [shaped(blocks, bf16), shaped(blocks, f32), shaped(blocks, bf16)],
            [pltpu.VMEM((basis_count, atoms, atoms), bf16)],
            smem,
            (pos, send_tab, feat_tab, radial[0], update_t[0], w_send[1].T),
        )
        s2 = flat(padded(grid_of(s2_own)))
        g2, dh2, ds = call(
            functools.partial(second_kernel, target_of),
            [shaped(blocks, bf16), shaped(blocks, f32), shaped(ext_count, bf16)],
            [
                pltpu.VMEM((src.shape[1], basis_count, atoms, atoms), bf16),
                pltpu.VMEM((ext_count, channels, atoms), f32),
            ],
            smem,
            (pos, s2, h1, radial[1], w_update[1], update_t[1], w_out, w_out.T, energy),
        )
        ds_own = flat(folded(ds.reshape(ext_shape + ds.shape[1:])))
        (grad,) = call(
            functools.partial(third_kernel, target_of),
            [jax.ShapeDtypeStruct((ext_count, 8, atoms), f32)],
            [
                pltpu.VMEM((2 * channels, basis_count * atoms), bf16),
                pltpu.VMEM((atoms, basis_count * atoms), f32),
            ],
            smem,
            (pos, s2, g2, dh2, ds_own, u1, send_tab, radial[0], radial[1], w_send[1], w_update[0]),
        )
        total = folded(grad.reshape(ext_shape + grad.shape[1:]))
        return -total[..., :3, :]

    mass = jnp.zeros(species.shape, f32)
    for s in range(kinds):
        mass = jnp.where(species == s, masses[s], mass)
    mass = mass[..., None, :]
    inverse = 1.0 / mass
    force_now = forces(positions)
    half_kick = velocities + 0.5 * time_step * force_now * inverse
    travelled = time_step * half_kick
    coords = positions + travelled
    force_now = forces(coords)
    velocity = half_kick + 0.5 * time_step * force_now * inverse
    real_here = (species > 0).astype(f32)[..., None, :]
    local_kinetic = jnp.sum(real_here * 0.5 * mass * velocity * velocity)
    kinetic = lax.psum(local_kinetic, ("gx", "gy", "gz"))
    slot_total = (
        positions.size // 3 * lax.axis_size("gx") * lax.axis_size("gy") * lax.axis_size("gz")
    )
    factor = jnp.sqrt(target_slot * slot_total / (kinetic + tiny_eps))
    return (travelled, velocity * factor)


def solution(mesh):
    placed = (
        P("gx", "gy", "gz", None, None),
        P("gx", "gy", "gz", None, None),
        P("gx", "gy", "gz", None),
        P("gx", "gy", "gz", None),
        P(),
        P(),
        P(),
        P(),
        P(),
        P(),
        P(),
    )
    return jax.shard_map(
        local,
        mesh=mesh,
        in_specs=placed,
        out_specs=(P("gx", "gy", "gz", None, None), P("gx", "gy", "gz", None, None)),
        check_vma=False,
    )
```

time: 1180 us -> 459 us (0.39); the launches traced: 1160 us -> 456 us
  local copies, waits for them, and re-layouts: 362 us -> 4.58 us
  matrix products: 233 us -> 0.12 us
  other arithmetic: 219 us -> 6.47 us
  Pallas kernels: 0 us -> 148 us
  loops' own time: 101 us -> 0 us
  waiting for transfers between devices: 29.1 us -> 116 us
  starting transfers between devices: 168 us -> 136 us
    dot_general x210 -> x1, matrix products: 233 us -> 0.12 us  [local(): jnp.dot(embedding, w_send[0], preferred_element_type=f32).astype(bf16)]
    gather x144 -> x0, local copies, waits for them, and re-layouts: 171 us -> none  [the longest x48 73.3 us: one_block(): jnp.take(flat_feat, source_idx, axis=0)]
    pallas_call x0 -> x6, Pallas kernels: none -> 148 us  [call(): pl.pallas_call(kernel, out_shape=outs, in_specs=[pl.BlockSpec(memory_spac...]
    another operation x6 -> x0, loops' own time: 101 us -> none  [the longest x4 67.8 us: layer_one(): layer_out = lax.map(jax.checkpoint(one_block), tables)]
    ppermute x54 -> x48, waiting for transfers between devices: 29.1 us -> 116 us  [the longest x12 49.9 us: padded(): lax.ppermute(head, axis, [(i + 1, i) for i in range(ends)])]
    add_any x128 -> x0, other arithmetic: 69.2 us -> none  [the longest x32 54.2 us: layer_two_energy(): return jnp.sum(lax.map(jax.checkpoint(one_block), tables))]
    dynamic_slice x48 -> x0, local copies, waits for them, and re-layouts: 62.7 us -> none  [layer_one(): layer_out = lax.map(jax.checkpoint(one_block), tables)]
    squeeze x82 -> x3, local copies, waits for them, and re-layouts: 57.2 us -> 0.01 us  [the longest x1 0.01 us: forces(): w_send[1]]
  transfers between devices with their start and end apart: 54 -> 48, of which waited for: 29 -> 41; matrix products, arithmetic and copies ran while one was open for 1% -> 1% of each run, Pallas kernels for 0% -> 0%
where the time goes in v1:
time: 459 us; the launch traced here: 456 us
  Pallas kernels  148 us (32%)
  starting transfers between devices  136 us (30%)
  waiting for transfers between devices  116 us (25%)
  blocking collectives  43 us (9%)
  other arithmetic  6.47 us (1%)
    pallas_call x6, Pallas kernels, call(): pl.pallas_call(kernel, out_shape=outs, in_specs=[pl.BlockSpec(memory_spac...  148 us
    ppermute x12, starting transfers between devices, folded(): from_low = lax.ppermute(high, axis, [(i, i + 1) for i in range(ends)])  64 us
    ppermute x12, waiting for transfers between devices, padded(): lax.ppermute(head, axis, [(i + 1, i) for i in range(ends)])  49.9 us
    ppermute x12, waiting for transfers between devices, folded(): from_high = lax.ppermute(low, axis, [(i + 1, i) for i in range(ends)])  44.4 us
    psum x1, blocking collectives, local(): kinetic = lax.psum(local_kinetic, ('gx', 'gy', 'gz'))  43 us
    ppermute x12, starting transfers between devices, padded(): lax.ppermute(tail, axis, [(i, i + 1) for i in range(ends)])  40.6 us
    ppermute x12, waiting for transfers between devices, folded(): from_low = lax.ppermute(high, axis, [(i, i + 1) for i in range(ends)])  17.8 us
    ppermute x12, starting transfers between devices, padded(): lax.ppermute(head, axis, [(i + 1, i) for i in range(ends)])  15.5 us
  transfers between devices with their start and end apart: 48, of which 41 were waited for; matrix products, arithmetic and copies ran while one was open for 1% of the time, Pallas kernels for 0%

profile of v1, /device:TPU:0, one launch (start us, length us, event | category | flops | bytes accessed | tf_op | source)
XLA Modules:
  0.0 456.3 jit_solution(6857018474001307577)
XLA Ops:
  2.1 5.0 %collective-permute-start = (f32[1,2,2,8,128]{4,3,2,1,0:T(8,128)S(1)}, f32[1,2,2,8,128]{4,3,2,1,0:T(8,128)S(1)}, u32[]{:S(2)}, u32[]{:S(2)}) collective-permute-start(f32[1,2,2,8,128]{4,3,2,1,0:T(8,128)S(1)} %get-tuple-element.86), channel_id=1, source_target_pairs={{0,8},{8,16},{16,24},{1,9},{9,17},{17,25},{2,10},{10,18},{18,26},{... | collective-permute-start | bytes 49160 | tf_op jit(solution)/shard_map/ppermute | solution.py:33
  17.8 4.2 collective-permute-done.3
  28.6 20.6 %shard_map.131 = (bf16[8,64,128]{2,1,0:T(8,128)(2,1)S(1)}, f32[8,64,128]{2,1,0:T(8,128)S(1)}, bf16[8,64,128]{2,1,0:T(8,128)(2,1)S(1)}) custom-call(s32[8,8]{1,0:T(8,128)S(1)} %bitcast.82, s32[8]{0:T(128)S(1)} %reshape.65.live, f32[64,8,128]{2,1,0:T(8,128)S(1)} %bitcast.60, f32[4,64,128]{2,1,0:T(8,128)S(1)} %broadcast_in_dim.62.send_tab, ...), custom_call_target="tpu_custom_call" | custom-call | tf_op jit(solution)/shard_map/pallas_call | solution.py:269
  54.6 4.3 collective-permute-done.7
  64.9 4.4 collective-permute-done.9
  69.4 5.2 %collective-permute-start.10 = (bf16[4,4,1,64,128]{4,3,2,1,0:T(8,128)(2,1)S(1)}, bf16[4,4,1,64,128]{4,3,2,1,0:T(8,128)(2,1)S(1)}, u32[]{:S(2)}, u32[]{:S(2)}) collective-permute-start(bf16[4,4,1,64,128]{4,3,2,1,0:T(8,128)(2,1)S(1)} %get-tuple-element.40), channel_id=1, source_target_pairs={{0,1},{1,2},{2,3},{4,5},{5,6},{6,7},{8,9},{9,10},{10,11},{12,13},{... | collective-permute-start | bytes 786440 | tf_op jit(solution)/shard_map/ppermute | solution.py:33
  80.0 31.3 %shard_map.132 = (bf16[8,64,128]{2,1,0:T(8,128)(2,1)S(1)}, f32[8,64,128]{2,1,0:T(8,128)S(1)}, bf16[64,64,128]{2,1,0:T(8,128)(2,1)S(1)}) custom-call(s32[8,8]{1,0:T(8,128)S(1)} %bitcast.83, s32[8]{0:T(128)S(1)} %reshape.65.live, f32[64,8,128]{2,1,0:T(8,128)S(1)} %bitcast.61, bf16[64,64,128]{2,1,0:T(8,128)(2,1)S(1)} %bitcast.58, ...), custom_call_target="tpu_custom_call" | custom-call | tf_op jit(solution)/shard_map/pallas_call | solution.py:269
  111.4 6.0 %collective-permute-start.12 = (bf16[4,4,1,64,128]{4,3,2,1,0:T(8,128)(2,1)S(1)}, bf16[4,4,1,64,128]{4,3,2,1,0:T(8,128)(2,1)S(1)}, u32[]{:S(2)}, u32[]{:S(2)}) collective-permute-start(bf16[4,4,1,64,128]{4,3,2,1,0:T(8,128)(2,1)S(1)} %slice.427), channel_id=1, source_target_pairs={{0,1},{1,2},{2,3},{4,5},{5,6},{6,7},{8,9},{9,10},{10,11},{12,13},{... | collective-permute-start | bytes 786440 | tf_op jit(solution)/shard_map/ppermute | solution.py:49
  128.9 5.6 %collective-permute-done.15 = bf16[4,1,2,64,128]{4,3,2,1,0:T(8,128)(2,1)S(1)} collective-permute-done((bf16[4,1,2,64,128]{4,3,2,1,0:T(8,128)(2,1)S(1)}, bf16[4,1,2,64,128]{4,3,2,1,0:T(8,128)(2,1)S(1)}, u32[]{:S(2)}, u32[]{:S(2)}) %collective-permute-start.15) | collective-permute-done | bytes 131104 | tf_op jit(solution)/shard_map/ppermute | solution.py:50
  134.5 10.0 %collective-permute-start.16 = (bf16[1,2,2,64,128]{4,3,2,1,0:T(8,128)(2,1)S(1)}, bf16[1,2,2,64,128]{4,3,2,1,0:T(8,128)(2,1)S(1)}, u32[]{:S(2)}, u32[]{:S(2)}) collective-permute-start(bf16[1,2,2,64,128]{4,3,2,1,0:T(8,128)(2,1)S(1)} %fusion.44), channel_id=1, source_target_pairs={{0,8},{8,16},{16,24},{1,9},{9,17},{17,25},{2,10},{10,18},{18,26},{... | collective-permute-start | bytes 196616 | tf_op jit(solution)/shard_map/ppermute | solution.py:49
  147.6 5.2 %collective-permute-done.17 = bf16[1,2,2,64,128]{4,3,2,1,0:T(8,128)(2,1)S(1)} collective-permute-done((bf16[1,2,2,64,128]{4,3,2,1,0:T(8,128)(2,1)S(1)}, bf16[1,2,2,64,128]{4,3,2,1,0:T(8,128)(2,1)S(1)}, u32[]{:S(2)}, u32[]{:S(2)}) %collective-permute-start.17) | collective-permute-done | bytes 65568 | tf_op jit(solution)/shard_map/ppermute | solution.py:50
  152.9 22.0 %shard_map.133 = f32[64,8,128]{2,1,0:T(8,128)S(1)} custom-call(s32[8,8]{1,0:T(8,128)S(1)} %bitcast.84, s32[8]{0:T(128)S(1)} %reshape.65.live, f32[64,8,128]{2,1,0:T(8,128)S(1)} %bitcast.62, bf16[64,64,128]{2,1,0:T(8,128)(2,1)S(1)} %bitcast.59, bf16[8,64,128]{2,1,0:T(8,128)(2,1)S(1)} %get-tuple-element.16.g2, f32[8,64,128]{2,1,0:T(8,128)S(1)} %get-tuple-element.17.dh2, ...), custom_call_target="tpu_custom_call" | custom-call | tf_op jit(solution)/shard_map/pallas_call | solution.py:269
  185.6 4.5 collective-permute-done.21
  190.2 9.3 %collective-permute-start.22 = (f32[1,2,2,8,128]{4,2,3,1,0:T(2,128)S(1)}, f32[1,2,2,8,128]{4,2,3,1,0:T(2,128)S(1)}, u32[]{:S(2)}, u32[]{:S(2)}) collective-permute-start(f32[1,2,2,8,128]{4,2,3,1,0:T(2,128)S(1)} %fusion.60), channel_id=1, source_target_pairs={{0,8},{8,16},{16,24},{1,9},{9,17},{17,25},{2,10},{10,18},{18,26},{... | collective-permute-start | bytes 49160 | tf_op jit(solution)/shard_map/ppermute | solution.py:49
  212.4 4.2 collective-permute-done.25
  219.7 4.2 collective-permute-done.27
  226.6 7.3 %collective-permute-done.29 = f32[4,4,1,8,128]{4,3,2,1,0:T(8,128)S(1)} collective-permute-done((f32[4,4,1,8,128]{4,3,2,1,0:T(8,128)S(1)}, f32[4,4,1,8,128]{4,3,2,1,0:T(8,128)S(1)}, u32[]{:S(2)}, u32[]{:S(2)}) %collective-permute-start.29) | collective-permute-done | bytes 65568 | tf_op jit(solution)/shard_map/ppermute | solution.py:35
  233.9 20.6 %shard_map.134 = (bf16[8,64,128]{2,1,0:T(8,128)(2,1)S(1)}, f32[8,64,128]{2,1,0:T(8,128)S(1)}, bf16[8,64,128]{2,1,0:T(8,128)(2,1)S(1)}) custom-call(s32[8,8]{1,0:T(8,128)S(1)} %bitcast.85, s32[8]{0:T(128)S(1)} %reshape.65.live, f32[64,8,128]{2,1,0:T(8,128)S(1)} %bitcast.63, f32[4,64,128]{2,1,0:T(8,128)S(1)} %broadcast_in_dim.62.send_tab, ...), custom_call_target="tpu_custom_call" | custom-call | tf_op jit(solution)/shard_map/pallas_call | solution.py:269
  259.9 4.3 collective-permute-done.31
  264.3 4.0 collective-permute-start.32
  270.8 4.4 collective-permute-done.33
  275.3 4.6 %collective-permute-start.34 = (bf16[4,4,1,64,128]{4,3,2,1,0:T(8,128)(2,1)S(1)}, bf16[4,4,1,64,128]{4,3,2,1,0:T(8,128)(2,1)S(1)}, u32[]{:S(2)}, u32[]{:S(2)}) collective-permute-start(bf16[4,4,1,64,128]{4,3,2,1,0:T(8,128)(2,1)S(1)} %get-tuple-element.36), channel_id=1, source_target_pairs={{0,1},{1,2},{2,3},{4,5},{5,6},{6,7},{8,9},{9,10},{10,11},{12,13},{... | collective-permute-start | bytes 786440 | tf_op jit(solution)/shard_map/ppermute | solution.py:33
  284.4 31.3 %shard_map.135 = (bf16[8,64,128]{2,1,0:T(8,128)(2,1)S(1)}, f32[8,64,128]{2,1,0:T(8,128)S(1)}, bf16[64,64,128]{2,1,0:T(8,128)(2,1)S(1)}) custom-call(s32[8,8]{1,0:T(8,128)S(1)} %bitcast.86, s32[8]{0:T(128)S(1)} %reshape.65.live, f32[64,8,128]{2,1,0:T(8,128)S(1)} %bitcast.64, bf16[64,64,128]{2,1,0:T(8,128)(2,1)S(1)} %bitcast.56, ...), custom_call_target="tpu_custom_call" | custom-call | tf_op jit(solution)/shard_map/pallas_call | solution.py:269
  315.8 6.0 %collective-permute-start.36 = (bf16[4,4,1,64,128]{4,3,2,1,0:T(8,128)(2,1)S(1)}, bf16[4,4,1,64,128]{4,3,2,1,0:T(8,128)(2,1)S(1)}, u32[]{:S(2)}, u32[]{:S(2)}) collective-permute-start(bf16[4,4,1,64,128]{4,3,2,1,0:T(8,128)(2,1)S(1)} %slice.469), channel_id=1, source_target_pairs={{0,1},{1,2},{2,3},{4,5},{5,6},{6,7},{8,9},{9,10},{10,11},{12,13},{... | collective-permute-start | bytes 786440 | tf_op jit(solution)/shard_map/ppermute | solution.py:49
  333.3 5.6 %collective-permute-done.39 = bf16[4,1,2,64,128]{4,3,2,1,0:T(8,128)(2,1)S(1)} collective-permute-done((bf16[4,1,2,64,128]{4,3,2,1,0:T(8,128)(2,1)S(1)}, bf16[4,1,2,64,128]{4,3,2,1,0:T(8,128)(2,1)S(1)}, u32[]{:S(2)}, u32[]{:S(2)}) %collective-permute-start.39) | collective-permute-done | bytes 131104 | tf_op jit(solution)/shard_map/ppermute | solution.py:50
  338.9 10.0 %collective-permute-start.40 = (bf16[1,2,2,64,128]{4,3,2,1,0:T(8,128)(2,1)S(1)}, bf16[1,2,2,64,128]{4,3,2,1,0:T(8,128)(2,1)S(1)}, u32[]{:S(2)}, u32[]{:S(2)}) collective-permute-start(bf16[1,2,2,64,128]{4,3,2,1,0:T(8,128)(2,1)S(1)} %fusion.39), channel_id=1, source_target_pairs={{0,8},{8,16},{16,24},{1,9},{9,17},{17,25},{2,10},{10,18},{18,26},{... | collective-permute-start | bytes 196616 | tf_op jit(solution)/shard_map/ppermute | solution.py:49
  352.1 5.2 %collective-permute-done.41 = bf16[1,2,2,64,128]{4,3,2,1,0:T(8,128)(2,1)S(1)} collective-permute-done((bf16[1,2,2,64,128]{4,3,2,1,0:T(8,128)(2,1)S(1)}, bf16[1,2,2,64,128]{4,3,2,1,0:T(8,128)(2,1)S(1)}, u32[]{:S(2)}, u32[]{:S(2)}) %collective-permute-start.41) | collective-permute-done | bytes 65568 | tf_op jit(solution)/shard_map/ppermute | solution.py:50
  357.3 22.0 %shard_map.136 = f32[64,8,128]{2,1,0:T(8,128)S(1)} custom-call(s32[8,8]{1,0:T(8,128)S(1)} %bitcast.87, s32[8]{0:T(128)S(1)} %reshape.65.live, f32[64,8,128]{2,1,0:T(8,128)S(1)} %bitcast.65, bf16[64,64,128]{2,1,0:T(8,128)(2,1)S(1)} %bitcast.57, bf16[8,64,128]{2,1,0:T(8,128)(2,1)S(1)} %get-tuple-element.22.g2, f32[8,64,128]{2,1,0:T(8,128)S(1)} %get-tuple-element.23.dh2, ...), custom_call_target="tpu_custom_call" | custom-call | tf_op jit(solution)/shard_map/pallas_call | solution.py:269
  390.1 4.5 collective-permute-done.45
  394.6 9.1 %collective-permute-start.46 = (f32[1,2,2,8,128]{4,2,3,1,0:T(2,128)S(1)}, f32[1,2,2,8,128]{4,2,3,1,0:T(2,128)S(1)}, u32[]{:S(2)}, u32[]{:S(2)}) collective-permute-start(f32[1,2,2,8,128]{4,2,3,1,0:T(2,128)S(1)} %fusion.57), channel_id=1, source_target_pairs={{0,8},{8,16},{16,24},{1,9},{9,17},{17,25},{2,10},{10,18},{18,26},{... | collective-permute-start | bytes 49160 | tf_op jit(solution)/shard_map/ppermute | solution.py:49
  406.5 4.8 %collective-permute-done.47 = f32[1,2,2,8,128]{4,2,3,1,0:T(2,128)S(1)} collective-permute-done((f32[1,2,2,8,128]{4,2,3,1,0:T(2,128)S(1)}, f32[1,2,2,8,128]{4,2,3,1,0:T(2,128)S(1)}, u32[]{:S(2)}, u32[]{:S(2)}) %collective-permute-start.47) | collective-permute-done | bytes 16416 | tf_op jit(solution)/shard_map/ppermute | solution.py:50
  411.9 43.0 %psum.7 = f32[]{:T(128)} all-reduce(f32[]{:T(128)} %get-tuple-element.26), channel_id=1, replica_groups=mesh['gx'=4,'gy'=2,'gz'=4] {'gx','gy','gz'}, use_global_device_ids=true, to_apply=%region_2.3 | all-reduce | flops 1 | bytes 8 | tf_op jit(solution)/shard_map/psum | solution.py:377
  (186 shorter events, 121.3 us)
Async XLA Ops:
  2.1 7.3 %collective-permute-start = (f32[1,2,2,8,128]{4,3,2,1,0:T(8,128)S(1)}, f32[1,2,2,8,128]{4,3,2,1,0:T(8,128)S(1)}, u32[]{:S(2)}, u32[]{:S(2)}) collective-permute-start(f32[1,2,2,8,128]{4,3,2,1,0:T(8,128)S(1)} %get-tuple-element.86), channel_id=1, source_target_pairs={{0,8},{8,16},{16,24},{1,9},{9,17},{17,25},{2,10},{10,18},{18,26},{... | collective-permute-start | bytes 49160 | tf_op jit(solution)/shard_map/ppermute | solution.py:33
  7.1 5.6 %collective-permute-start.1 = (f32[1,2,2,8,128]{4,3,2,1,0:T(8,128)S(1)}, f32[1,2,2,8,128]{4,3,2,1,0:T(8,128)S(1)}, u32[]{:S(2)}, u32[]{:S(2)}) collective-permute-start(f32[1,2,2,8,128]{4,3,2,1,0:T(8,128)S(1)} %get-tuple-element.87), channel_id=1, source_target_pairs={{8,0},{16,8},{24,16},{9,1},{17,9},{25,17},{10,2},{18,10},{26,18},{... | collective-permute-start | bytes 49160 | tf_op jit(solution)/shard_map/ppermute | solution.py:35
  16.2 5.8 %collective-permute-start.3 = (f32[4,1,2,8,128]{4,3,2,1,0:T(8,128)S(1)}, f32[4,1,2,8,128]{4,3,2,1,0:T(8,128)S(1)}, u32[]{:S(2)}, u32[]{:S(2)}) collective-permute-start(f32[4,1,2,8,128]{4,3,2,1,0:T(8,128)S(1)} %get-tuple-element.77), channel_id=1, source_target_pairs={{4,0},{5,1},{6,2},{7,3},{12,8},{13,9},{14,10},{15,11},{20,16},{21,... | collective-permute-start | bytes 98312 | tf_op jit(solution)/shard_map/ppermute | solution.py:35
  49.2 5.4 %collective-permute-start.6 = (bf16[1,2,2,64,128]{4,3,2,1,0:T(8,128)(2,1)S(1)}, bf16[1,2,2,64,128]{4,3,2,1,0:T(8,128)(2,1)S(1)}, u32[]{:S(2)}, u32[]{:S(2)}) collective-permute-start(bf16[1,2,2,64,128]{4,3,2,1,0:T(8,128)(2,1)S(1)} %bitcast.105), channel_id=1, source_target_pairs={{0,8},{8,16},{16,24},{1,9},{9,17},{17,25},{2,10},{10,18},{18,26},{... | collective-permute-start | bytes 196616 | tf_op jit(solution)/shard_map/ppermute | solution.py:33
  52.7 6.2 %collective-permute-start.7 = (bf16[1,2,2,64,128]{4,3,2,1,0:T(8,128)(2,1)S(1)}, bf16[1,2,2,64,128]{4,3,2,1,0:T(8,128)(2,1)S(1)}, u32[]{:S(2)}, u32[]{:S(2)}) collective-permute-start(bf16[1,2,2,64,128]{4,3,2,1,0:T(8,128)(2,1)S(1)} %bitcast.103), channel_id=1, source_target_pairs={{8,0},{16,8},{24,16},{9,1},{17,9},{25,17},{10,2},{18,10},{26,18},{... | collective-permute-start | bytes 196616 | tf_op jit(solution)/shard_map/ppermute | solution.py:35
  58.9 6.0 %collective-permute-start.8 = (bf16[4,1,2,64,128]{4,3,2,1,0:T(8,128)(2,1)S(1)}, bf16[4,1,2,64,128]{4,3,2,1,0:T(8,128)(2,1)S(1)}, u32[]{:S(2)}, u32[]{:S(2)}) collective-permute-start(bf16[4,1,2,64,128]{4,3,2,1,0:T(8,128)(2,1)S(1)} %get-tuple-element.56), channel_id=1, source_target_pairs={{0,4},{1,5},{2,6},{3,7},{8,12},{9,13},{10,14},{11,15},{16,20},{17,... | collective-permute-start | bytes 393224 | tf_op jit(solution)/shard_map/ppermute | solution.py:33
  62.4 6.9 %collective-permute-start.9 = (bf16[4,1,2,64,128]{4,3,2,1,0:T(8,128)(2,1)S(1)}, bf16[4,1,2,64,128]{4,3,2,1,0:T(8,128)(2,1)S(1)}, u32[]{:S(2)}, u32[]{:S(2)}) collective-permute-start(bf16[4,1,2,64,128]{4,3,2,1,0:T(8,128)(2,1)S(1)} %get-tuple-element.57), channel_id=1, source_target_pairs={{4,0},{5,1},{6,2},{7,3},{12,8},{13,9},{14,10},{15,11},{20,16},{21,... | collective-permute-start | bytes 393224 | tf_op jit(solution)/shard_map/ppermute | solution.py:35
  69.4 6.6 %collective-permute-start.10 = (bf16[4,4,1,64,128]{4,3,2,1,0:T(8,128)(2,1)S(1)}, bf16[4,4,1,64,128]{4,3,2,1,0:T(8,128)(2,1)S(1)}, u32[]{:S(2)}, u32[]{:S(2)}) collective-permute-start(bf16[4,4,1,64,128]{4,3,2,1,0:T(8,128)(2,1)S(1)} %get-tuple-element.40), channel_id=1, source_target_pairs={{0,1},{1,2},{2,3},{4,5},{5,6},{6,7},{8,9},{9,10},{10,11},{12,13},{... | collective-permute-start | bytes 786440 | tf_op jit(solution)/shard_map/ppermute | solution.py:33
  111.4 7.1 %collective-permute-start.12 = (bf16[4,4,1,64,128]{4,3,2,1,0:T(8,128)(2,1)S(1)}, bf16[4,4,1,64,128]{4,3,2,1,0:T(8,128)(2,1)S(1)}, u32[]{:S(2)}, u32[]{:S(2)}) collective-permute-start(bf16[4,4,1,64,128]{4,3,2,1,0:T(8,128)(2,1)S(1)} %slice.427), channel_id=1, source_target_pairs={{0,1},{1,2},{2,3},{4,5},{5,6},{6,7},{8,9},{9,10},{10,11},{12,13},{... | collective-permute-start | bytes 786440 | tf_op jit(solution)/shard_map/ppermute | solution.py:49
  127.6 6.9 %collective-permute-start.15 = (bf16[4,1,2,64,128]{4,3,2,1,0:T(8,128)(2,1)S(1)}, bf16[4,1,2,64,128]{4,3,2,1,0:T(8,128)(2,1)S(1)}, u32[]{:S(2)}, u32[]{:S(2)}) collective-permute-start(bf16[4,1,2,64,128]{4,3,2,1,0:T(8,128)(2,1)S(1)} %get-tuple-element.39), channel_id=1, source_target_pairs={{4,0},{5,1},{6,2},{7,3},{12,8},{13,9},{14,10},{15,11},{20,16},{21,... | collective-permute-start | bytes 393224 | tf_op jit(solution)/shard_map/ppermute | solution.py:50
  134.5 11.9 %collective-permute-start.16 = (bf16[1,2,2,64,128]{4,3,2,1,0:T(8,128)(2,1)S(1)}, bf16[1,2,2,64,128]{4,3,2,1,0:T(8,128)(2,1)S(1)}, u32[]{:S(2)}, u32[]{:S(2)}) collective-permute-start(bf16[1,2,2,64,128]{4,3,2,1,0:T(8,128)(2,1)S(1)} %fusion.44), channel_id=1, source_target_pairs={{0,8},{8,16},{16,24},{1,9},{9,17},{17,25},{2,10},{10,18},{18,26},{... | collective-permute-start | bytes 196616 | tf_op jit(solution)/shard_map/ppermute | solution.py:49
  146.3 6.5 %collective-permute-start.17 = (bf16[1,2,2,64,128]{4,3,2,1,0:T(8,128)(2,1)S(1)}, bf16[1,2,2,64,128]{4,3,2,1,0:T(8,128)(2,1)S(1)}, u32[]{:S(2)}, u32[]{:S(2)}) collective-permute-start(bf16[1,2,2,64,128]{4,3,2,1,0:T(8,128)(2,1)S(1)} %get-tuple-element.55), channel_id=1, source_target_pairs={{8,0},{16,8},{24,16},{9,1},{17,9},{25,17},{10,2},{18,10},{26,18},{... | collective-permute-start | bytes 196616 | tf_op jit(solution)/shard_map/ppermute | solution.py:50
  184.3 5.8 %collective-permute-start.21 = (f32[4,1,2,8,128]{4,2,3,1,0:T(2,128)S(1)}, f32[4,1,2,8,128]{4,2,3,1,0:T(2,128)S(1)}, u32[]{:S(2)}, u32[]{:S(2)}) collective-permute-start(f32[4,1,2,8,128]{4,2,3,1,0:T(2,128)S(1)} %get-tuple-element.65), channel_id=1, source_target_pairs={{4,0},{5,1},{6,2},{7,3},{12,8},{13,9},{14,10},{15,11},{20,16},{21,... | collective-permute-start | bytes 98312 | tf_op jit(solution)/shard_map/ppermute | solution.py:50
  190.2 10.6 %collective-permute-start.22 = (f32[1,2,2,8,128]{4,2,3,1,0:T(2,128)S(1)}, f32[1,2,2,8,128]{4,2,3,1,0:T(2,128)S(1)}, u32[]{:S(2)}, u32[]{:S(2)}) collective-permute-start(f32[1,2,2,8,128]{4,2,3,1,0:T(2,128)S(1)} %fusion.60), channel_id=1, source_target_pairs={{0,8},{8,16},{16,24},{1,9},{9,17},{17,25},{2,10},{10,18},{18,26},{... | collective-permute-start | bytes 49160 | tf_op jit(solution)/shard_map/ppermute | solution.py:49
  200.8 6.1 %collective-permute-start.23 = (f32[1,2,2,8,128]{4,2,3,1,0:T(2,128)S(1)}, f32[1,2,2,8,128]{4,2,3,1,0:T(2,128)S(1)}, u32[]{:S(2)}, u32[]{:S(2)}) collective-permute-start(f32[1,2,2,8,128]{4,2,3,1,0:T(2,128)S(1)} %get-tuple-element.75), channel_id=1, source_target_pairs={{8,0},{16,8},{24,16},{9,1},{17,9},{25,17},{10,2},{18,10},{26,18},{... | collective-permute-start | bytes 49160 | tf_op jit(solution)/shard_map/ppermute | solution.py:50
  207.0 5.4 %collective-permute-start.24 = (f32[1,2,2,8,128]{4,3,2,1,0:T(8,128)S(1)}, f32[1,2,2,8,128]{4,3,2,1,0:T(8,128)S(1)}, u32[]{:S(2)}, u32[]{:S(2)}) collective-permute-start(f32[1,2,2,8,128]{4,3,2,1,0:T(8,128)S(1)} %get-tuple-element.78), channel_id=1, source_target_pairs={{0,8},{8,16},{16,24},{1,9},{9,17},{17,25},{2,10},{10,18},{18,26},{... | collective-permute-start | bytes 49160 | tf_op jit(solution)/shard_map/ppermute | solution.py:33
  210.9 5.6 %collective-permute-start.25 = (f32[1,2,2,8,128]{4,3,2,1,0:T(8,128)S(1)}, f32[1,2,2,8,128]{4,3,2,1,0:T(8,128)S(1)}, u32[]{:S(2)}, u32[]{:S(2)}) collective-permute-start(f32[1,2,2,8,128]{4,3,2,1,0:T(8,128)S(1)} %get-tuple-element.79), channel_id=1, source_target_pairs={{8,0},{16,8},{24,16},{9,1},{17,9},{25,17},{10,2},{18,10},{26,18},{... | collective-permute-start | bytes 49160 | tf_op jit(solution)/shard_map/ppermute | solution.py:35
  218.1 5.8 %collective-permute-start.27 = (f32[4,1,2,8,128]{4,3,2,1,0:T(8,128)S(1)}, f32[4,1,2,8,128]{4,3,2,1,0:T(8,128)S(1)}, u32[]{:S(2)}, u32[]{:S(2)}) collective-permute-start(f32[4,1,2,8,128]{4,3,2,1,0:T(8,128)S(1)} %get-tuple-element.73), channel_id=1, source_target_pairs={{4,0},{5,1},{6,2},{7,3},{12,8},{13,9},{14,10},{15,11},{20,16},{21,... | collective-permute-start | bytes 98312 | tf_op jit(solution)/shard_map/ppermute | solution.py:35
  225.2 8.6 %collective-permute-start.29 = (f32[4,4,1,8,128]{4,3,2,1,0:T(8,128)S(1)}, f32[4,4,1,8,128]{4,3,2,1,0:T(8,128)S(1)}, u32[]{:S(2)}, u32[]{:S(2)}) collective-permute-start(f32[4,4,1,8,128]{4,3,2,1,0:T(8,128)S(1)} %get-tuple-element.63), channel_id=1, source_target_pairs={{1,0},{2,1},{3,2},{5,4},{6,5},{7,6},{9,8},{10,9},{11,10},{13,12},{... | collective-permute-start | bytes 196616 | tf_op jit(solution)/shard_map/ppermute | solution.py:35
  254.6 5.4 %collective-permute-start.30 = (bf16[1,2,2,64,128]{4,3,2,1,0:T(8,128)(2,1)S(1)}, bf16[1,2,2,64,128]{4,3,2,1,0:T(8,128)(2,1)S(1)}, u32[]{:S(2)}, u32[]{:S(2)}) collective-permute-start(bf16[1,2,2,64,128]{4,3,2,1,0:T(8,128)(2,1)S(1)} %bitcast.106), channel_id=1, source_target_pairs={{0,8},{8,16},{16,24},{1,9},{9,17},{17,25},{2,10},{10,18},{18,26},{... | collective-permute-start | bytes 196616 | tf_op jit(solution)/shard_map/ppermute | solution.py:33
  258.0 6.2 %collective-permute-start.31 = (bf16[1,2,2,64,128]{4,3,2,1,0:T(8,128)(2,1)S(1)}, bf16[1,2,2,64,128]{4,3,2,1,0:T(8,128)(2,1)S(1)}, u32[]{:S(2)}, u32[]{:S(2)}) collective-permute-start(bf16[1,2,2,64,128]{4,3,2,1,0:T(8,128)(2,1)S(1)} %bitcast.104), channel_id=1, source_target_pairs={{8,0},{16,8},{24,16},{9,1},{17,9},{25,17},{10,2},{18,10},{26,18},{... | collective-permute-start | bytes 196616 | tf_op jit(solution)/shard_map/ppermute | solution.py:35
  264.3 6.5 %collective-permute-start.32 = (bf16[4,1,2,64,128]{4,3,2,1,0:T(8,128)(2,1)S(1)}, bf16[4,1,2,64,128]{4,3,2,1,0:T(8,128)(2,1)S(1)}, u32[]{:S(2)}, u32[]{:S(2)}) collective-permute-start(bf16[4,1,2,64,128]{4,3,2,1,0:T(8,128)(2,1)S(1)} %get-tuple-element.48), channel_id=1, source_target_pairs={{0,4},{1,5},{2,6},{3,7},{8,12},{9,13},{10,14},{11,15},{16,20},{17,... | collective-permute-start | bytes 393224 | tf_op jit(solution)/shard_map/ppermute | solution.py:33
  268.3 6.9 %collective-permute-start.33 = (bf16[4,1,2,64,128]{4,3,2,1,0:T(8,128)(2,1)S(1)}, bf16[4,1,2,64,128]{4,3,2,1,0:T(8,128)(2,1)S(1)}, u32[]{:S(2)}, u32[]{:S(2)}) collective-permute-start(bf16[4,1,2,64,128]{4,3,2,1,0:T(8,128)(2,1)S(1)} %get-tuple-element.49), channel_id=1, source_target_pairs={{4,0},{5,1},{6,2},{7,3},{12,8},{13,9},{14,10},{15,11},{20,16},{21,... | collective-permute-start | bytes 393224 | tf_op jit(solution)/shard_map/ppermute | solution.py:35
  275.3 5.9 %collective-permute-start.34 = (bf16[4,4,1,64,128]{4,3,2,1,0:T(8,128)(2,1)S(1)}, bf16[4,4,1,64,128]{4,3,2,1,0:T(8,128)(2,1)S(1)}, u32[]{:S(2)}, u32[]{:S(2)}) collective-permute-start(bf16[4,4,1,64,128]{4,3,2,1,0:T(8,128)(2,1)S(1)} %get-tuple-element.36), channel_id=1, source_target_pairs={{0,1},{1,2},{2,3},{4,5},{5,6},{6,7},{8,9},{9,10},{10,11},{12,13},{... | collective-permute-start | bytes 786440 | tf_op jit(solution)/shard_map/ppermute | solution.py:33
  315.8 7.1 %collective-permute-start.36 = (bf16[4,4,1,64,128]{4,3,2,1,0:T(8,128)(2,1)S(1)}, bf16[4,4,1,64,128]{4,3,2,1,0:T(8,128)(2,1)S(1)}, u32[]{:S(2)}, u32[]{:S(2)}) collective-permute-start(bf16[4,4,1,64,128]{4,3,2,1,0:T(8,128)(2,1)S(1)} %slice.469), channel_id=1, source_target_pairs={{0,1},{1,2},{2,3},{4,5},{5,6},{6,7},{8,9},{9,10},{10,11},{12,13},{... | collective-permute-start | bytes 786440 | tf_op jit(solution)/shard_map/ppermute | solution.py:49
  332.0 6.9 %collective-permute-start.39 = (bf16[4,1,2,64,128]{4,3,2,1,0:T(8,128)(2,1)S(1)}, bf16[4,1,2,64,128]{4,3,2,1,0:T(8,128)(2,1)S(1)}, u32[]{:S(2)}, u32[]{:S(2)}) collective-permute-start(bf16[4,1,2,64,128]{4,3,2,1,0:T(8,128)(2,1)S(1)} %get-tuple-element.35), channel_id=1, source_target_pairs={{4,0},{5,1},{6,2},{7,3},{12,8},{13,9},{14,10},{15,11},{20,16},{21,... | collective-permute-start | bytes 393224 | tf_op jit(solution)/shard_map/ppermute | solution.py:50
  338.9 11.9 %collective-permute-start.40 = (bf16[1,2,2,64,128]{4,3,2,1,0:T(8,128)(2,1)S(1)}, bf16[1,2,2,64,128]{4,3,2,1,0:T(8,128)(2,1)S(1)}, u32[]{:S(2)}, u32[]{:S(2)}) collective-permute-start(bf16[1,2,2,64,128]{4,3,2,1,0:T(8,128)(2,1)S(1)} %fusion.39), channel_id=1, source_target_pairs={{0,8},{8,16},{16,24},{1,9},{9,17},{17,25},{2,10},{10,18},{18,26},{... | collective-permute-start | bytes 196616 | tf_op jit(solution)/shard_map/ppermute | solution.py:49
  350.8 6.5 %collective-permute-start.41 = (bf16[1,2,2,64,128]{4,3,2,1,0:T(8,128)(2,1)S(1)}, bf16[1,2,2,64,128]{4,3,2,1,0:T(8,128)(2,1)S(1)}, u32[]{:S(2)}, u32[]{:S(2)}) collective-permute-start(bf16[1,2,2,64,128]{4,3,2,1,0:T(8,128)(2,1)S(1)} %get-tuple-element.47), channel_id=1, source_target_pairs={{8,0},{16,8},{24,16},{9,1},{17,9},{25,17},{10,2},{18,10},{26,18},{... | collective-permute-start | bytes 196616 | tf_op jit(solution)/shard_map/ppermute | solution.py:50
  379.3 5.1 %collective-permute-start.43 = (f32[4,4,1,8,128]{4,2,3,1,0:T(1,128)S(1)}, f32[4,4,1,8,128]{4,2,3,1,0:T(1,128)S(1)}, u32[]{:S(2)}, u32[]{:S(2)}) collective-permute-start(f32[4,4,1,8,128]{4,2,3,1,0:T(1,128)S(1)} %bitcast.110), channel_id=1, source_target_pairs={{1,0},{2,1},{3,2},{5,4},{6,5},{7,6},{9,8},{10,9},{11,10},{13,12},{... | collective-permute-start | bytes 196616 | tf_op jit(solution)/shard_map/ppermute | solution.py:50
  388.8 5.8 %collective-permute-start.45 = (f32[4,1,2,8,128]{4,2,3,1,0:T(2,128)S(1)}, f32[4,1,2,8,128]{4,2,3,1,0:T(2,128)S(1)}, u32[]{:S(2)}, u32[]{:S(2)}) collective-permute-start(f32[4,1,2,8,128]{4,2,3,1,0:T(2,128)S(1)} %get-tuple-element.59), channel_id=1, source_target_pairs={{4,0},{5,1},{6,2},{7,3},{12,8},{13,9},{14,10},{15,11},{20,16},{21,... | collective-permute-start | bytes 98312 | tf_op jit(solution)/shard_map/ppermute | solution.py:50
  394.6 10.6 %collective-permute-start.46 = (f32[1,2,2,8,128]{4,2,3,1,0:T(2,128)S(1)}, f32[1,2,2,8,128]{4,2,3,1,0:T(2,128)S(1)}, u32[]{:S(2)}, u32[]{:S(2)}) collective-permute-start(f32[1,2,2,8,128]{4,2,3,1,0:T(2,128)S(1)} %fusion.57), channel_id=1, source_target_pairs={{0,8},{8,16},{16,24},{1,9},{9,17},{17,25},{2,10},{10,18},{18,26},{... | collective-permute-start | bytes 49160 | tf_op jit(solution)/shard_map/ppermute | solution.py:49
  405.2 6.1 %collective-permute-start.47 = (f32[1,2,2,8,128]{4,2,3,1,0:T(2,128)S(1)}, f32[1,2,2,8,128]{4,2,3,1,0:T(2,128)S(1)}, u32[]{:S(2)}, u32[]{:S(2)}) collective-permute-start(f32[1,2,2,8,128]{4,2,3,1,0:T(2,128)S(1)} %get-tuple-element.71), channel_id=1, source_target_pairs={{8,0},{16,8},{24,16},{9,1},{17,9},{25,17},{10,2},{18,10},{26,18},{... | collective-permute-start | bytes 49160 | tf_op jit(solution)/shard_map/ppermute | solution.py:50
  (29 other events, 313.2 us)

commit v2 on v1

--- a/solution.py
+++ b/solution.py
@@ -22,41 +22,266 @@
 SIDES = (("gx", 0), ("gy", 1), ("gz", 2))
 
 
-def padded(cells):
-    for axis, dim in SIDES:
+MESH = pl.DeviceIdType.MESH
+
+
+def greet():
+    barrier = pltpu.get_barrier_semaphore()
+    places = []
+    expected = 0
+    for axis, _ in SIDES:
+        here = lax.axis_index(axis)
+        has_low, has_high = here > 0, here < lax.axis_size(axis) - 1
+        for there, present in ((here - 1, has_low), (here + 1, has_high)):
+
+            @pl.when(present)
+            def _(there=there, axis=axis):
+                pl.semaphore_signal(barrier, inc=1, device_id={axis: there}, device_id_type=MESH)
+
+        expected = expected + has_low.astype(jnp.int32) + has_high.astype(jnp.int32)
+        places.append((here, has_low, has_high))
+    pl.semaphore_wait(barrier, expected)
+    return places
+
+
+def swap(stage, place, low_pair, high_pair, send_sem, recv_sem):
+    axis = SIDES[stage][0]
+    here, has_low, has_high = place
+    sides = []
+    for way, (pair, there, present) in enumerate(
+        ((low_pair, here - 1, has_low), (high_pair, here + 1, has_high))
+    ):
+        copy = pltpu.make_async_remote_copy(
+            src_ref=pair[0],
+            dst_ref=pair[1],
+            send_sem=send_sem.at[stage, way],
+            recv_sem=recv_sem.at[stage, way],
+            device_id={axis: there},
+            device_id_type=MESH,
+        )
+        pl.when(present)(copy.start)
+        sides.append((copy, present))
+
+    def finish():
+        (to_low, has_low), (to_high, has_high) = sides
+        pl.when(has_low)(to_low.wait_send)
+        pl.when(has_high)(to_high.wait_send)
+        pl.when(has_high)(to_low.wait_recv)
+        pl.when(has_low)(to_high.wait_recv)
+
+    return finish
+
+
+def spans(sizes, dim, where, full):
+    index = []
+    for d, size in enumerate(sizes):
+        if d == dim:
+            index.append(pl.ds(where, 1))
+        elif d in full:
+            index.append(pl.ds(0, size + 2))
+        else:
+            index.append(pl.ds(1, size))
+    return tuple(index)
+
+
+def halo_kernel(own, ext, send_sem, recv_sem, copy_sem):
+    sizes = own.shape[:3]
+    inner = ext.at[tuple(pl.ds(1, size) for size in sizes)]
+    fill = pltpu.make_async_copy(own, inner, copy_sem)
+    fill.start()
+    for dim, (axis, _) in enumerate(SIDES):
+        here = lax.axis_index(axis)
+        for where, missing in (
+            (0, here == 0),
+            (sizes[dim] + 1, here == lax.axis_size(axis) - 1),
+        ):
+
+            @pl.when(missing)
+            def _(dim=dim, where=where):
+                index = spans(sizes, dim, where, range(dim))
+                shape = tuple(part.size for part in index) + ext.shape[3:]
+                ext[index] = jnp.zeros(shape, ext.dtype)
+
+    places = greet()
+    for dim in range(3):
+        size = sizes[dim]
+
+        def slab(where, full=range(dim), dim=dim):
+            return ext.at[spans(sizes, dim, where, full)]
+
+        if dim == 0:
+            low, high = own.at[pl.ds(0, 1)], own.at[pl.ds(size - 1, 1)]
+        else:
+            low, high = slab(1), slab(size)
+        finish = swap(
+            dim, places[dim], (low, slab(size + 1)), (high, slab(0)), send_sem, recv_sem
+        )
+        if dim == 0:
+            fill.wait()
+        finish()
+
+
+def fold_kernel(ext, own, *refs):
+    lands, sums = refs[:6], (ext,) + refs[6:8]
+    send_sem, recv_sem = refs[8:]
+    for stage in range(3):
+        dim = 2 - stage
+        axis = SIDES[dim][0]
+        here = lax.axis_index(axis)
+        for land, missing in (
+            (lands[2 * dim], here == 0),
+            (lands[2 * dim + 1], here == lax.axis_size(axis) - 1),
+        ):
+
+            @pl.when(missing)
+            def _(land=land):
+                land[...] = jnp.zeros_like(land)
+
+    places = greet()
+
+    def edge(source, dim, where):
+        return source.at[tuple(pl.ds(where, 1) if d == dim else slice(None) for d in range(3))]
+
+    def send(dim, source):
+        last = source.shape[dim] - 1
+        return swap(
+            dim,
+            places[dim],
+            (edge(source, dim, 0), lands[2 * dim + 1]),
+            (edge(source, dim, last), lands[2 * dim]),
+            send_sem,
+            recv_sem,
+        )
+
+    def total(source, dim, index):
+        size = source.shape[dim] - 2
+        place = index[dim]
+        moved = index[:dim] + (place + 1,) + index[dim + 1 :]
+        flat = index[:dim] + (0,) + index[dim + 1 :]
+        value = source[moved].astype(f32)
+        if place == 0:
+            value = value + lands[2 * dim][flat].astype(f32)
+        if place == size - 1:
+            value = value + lands[2 * dim + 1][flat].astype(f32)
+        return value.astype(own.dtype)
+
+    finish = send(2, ext)
+    for dim in (2, 1, 0):
+        source = sums[2 - dim]
+        finish()
+        target = own if dim == 0 else sums[3 - dim]
+        shape = target.shape[:3]
+        places_all = [
+            (x, y, z) for x in range(shape[0]) for y in range(shape[1]) for z in range(shape[2])
+        ]
+        rim = [i for i in places_all if dim > 0 and i[dim - 1] in (0, shape[dim - 1] - 1)]
+        for index in rim:
+            target[index] = total(source, dim, index)
+        if dim > 0:
+            finish = send(dim - 1, target)
+        for index in places_all:
+            if index not in rim:
+                target[index] = total(source, dim, index)
+
+
+def vmem_specs(count):
+    return [pl.BlockSpec(memory_space=pltpu.VMEM)] * count
+
+
+def remote(collective_id):
+    return pltpu.CompilerParams(
+        collective_id=collective_id, has_side_effects=True, vmem_limit_bytes=48 << 20
+    )
+
+
+def padded(cells, collective_id):
+    shape = tuple(size + 2 for size in cells.shape[:3]) + cells.shape[3:]
+    return pl.pallas_call(
+        halo_kernel,
+        out_shape=jax.ShapeDtypeStruct(shape, cells.dtype),
+        in_specs=vmem_specs(1),
+        out_specs=vmem_specs(1)[0],
+        scratch_shapes=[
+            pltpu.SemaphoreType.DMA((3, 2)),
+            pltpu.SemaphoreType.DMA((3, 2)),
+            pltpu.SemaphoreType.DMA,
+        ],
+        compiler_params=remote(collective_id),
+    )(cells)
+
+
+def folded(grid, collective_id):
+    x, y, z = (size - 2 for size in grid.shape[:3])
+    tail = grid.shape[3:]
+    landings = [(1, y, z), (1, y, z), (x + 2, 1, z), (x + 2, 1, z), (x + 2, y + 2, 1), (x + 2, y + 2, 1)]
+    sums = [(x + 2, y + 2, z), (x + 2, y, z)]
+    return pl.pallas_call(
+        fold_kernel,
+        out_shape=jax.ShapeDtypeStruct((x, y, z) + tail, grid.dtype),
+        in_specs=vmem_specs(1),
+        out_specs=vmem_specs(1)[0],
+        scratch_shapes=[pltpu.VMEM(shape + tail, grid.dtype) for shape in landings + sums]
+        + [pltpu.SemaphoreType.DMA((3, 2)), pltpu.SemaphoreType.DMA((3, 2))],
+        compiler_params=remote(collective_id),
+    )(grid)
+
+
+def thermostat_kernel(slot_total, part, velocity, out, *refs):
+    inbox, sums, (send_sem, recv_sem) = refs[:3], refs[3:6], refs[6:]
+    barrier = pltpu.get_barrier_semaphore()
+    peers = 0
+    for axis, _ in SIDES:
         count = lax.axis_size(axis)
-        ends = count - 1
-        head = lax.slice_in_dim(cells, 0, 1, axis=dim)
-        tail = lax.slice_in_dim(cells, cells.shape[dim] - 1, cells.shape[dim], axis=dim)
-        cells = jnp.concatenate(
-            [
-                lax.ppermute(tail, axis, [(i, i + 1) for i in range(ends)]),
-                cells,
-                lax.ppermute(head, axis, [(i + 1, i) for i in range(ends)]),
-            ],
-            axis=dim,
-        )
-    return cells
-
-
-def folded(grid):
-    for axis, dim in reversed(SIDES):
+        for t in range(1, count):
+            there = lax.rem(lax.axis_index(axis) + t, count)
+            pl.semaphore_signal(barrier, inc=1, device_id={axis: there}, device_id_type=MESH)
+            peers += 1
+    pl.semaphore_wait(barrier, peers)
+    current = part
+    base = 0
+    for stage, (axis, _) in enumerate(SIDES):
         count = lax.axis_size(axis)
-        ends = count - 1
-        size = grid.shape[dim]
-        low = lax.slice_in_dim(grid, 0, 1, axis=dim)
-        high = lax.slice_in_dim(grid, size - 1, size, axis=dim)
-        from_low = lax.ppermute(high, axis, [(i, i + 1) for i in range(ends)])
-        from_high = lax.ppermute(low, axis, [(i + 1, i) for i in range(ends)])
-        inner = lax.slice_in_dim(grid, 1, size - 1, axis=dim)
-        first = lax.slice_in_dim(inner, 0, 1, axis=dim) + from_low
-        last = lax.slice_in_dim(inner, size - 3, size - 2, axis=dim)
-        if size == 3:
-            grid = first + from_high
-        else:
-            middle = lax.slice_in_dim(inner, 1, size - 3, axis=dim)
-            grid = jnp.concatenate([first, middle, last + from_high], axis=dim)
-    return grid
+        copies = []
+        for t in range(1, count):
+            there = lax.rem(lax.axis_index(axis) + t, count)
+            copy = pltpu.make_async_remote_copy(
+                src_ref=current,
+                dst_ref=inbox[stage].at[t - 1],
+                send_sem=send_sem.at[base],
+                recv_sem=recv_sem.at[base],
+                device_id={axis: there},
+                device_id_type=MESH,
+            )
+            copy.start()
+            copies.append(copy)
+            base += 1
+        value = current[...]
+        for t, copy in enumerate(copies):
+            copy.wait()
+            value = value + inbox[stage][t]
+        sums[stage][...] = value
+        current = sums[stage]
+    kinetic = jnp.sum(value, keepdims=True)
+    factor = jnp.sqrt(target_slot * slot_total / (kinetic + tiny_eps))
+    for x in range(velocity.shape[0]):
+        for y in range(velocity.shape[1]):
+            for z in range(velocity.shape[2]):
+                out[x, y, z] = velocity[x, y, z] * factor
+
+
+def thermostat(part, velocity, slot_total, collective_id):
+    counts = [lax.axis_size(axis) for axis, _ in SIDES]
+    peers = sum(count - 1 for count in counts)
+    return pl.pallas_call(
+        functools.partial(thermostat_kernel, float(slot_total)),
+        out_shape=jax.ShapeDtypeStruct(velocity.shape, velocity.dtype),
+        in_specs=vmem_specs(2),
+        out_specs=vmem_specs(1)[0],
+        scratch_shapes=[pltpu.VMEM((max(count - 1, 1),) + part.shape, f32) for count in counts]
+        + [pltpu.VMEM(part.shape, f32)] * 3
+        + [pltpu.SemaphoreType.DMA((peers,)), pltpu.SemaphoreType.DMA((peers,))],
+        compiler_params=remote(collective_id),
+    )(part, velocity)
 
 
 def slot_tables(neighbour_blocks):
@@ -109,7 +334,8 @@
         powers[k] = powers[k - 1] * up
     for k in range(mid - 1, -1, -1):
         powers[k] = powers[k + 1] * down
-    return powers
+    scales = basis_constants(basis_count)[3]
+    return [power * scale if scale != 1.0 else power for power, scale in zip(powers, scales)]
 
 
 def fill_kernel(store, own, cols, is_self, basis_count):
@@ -117,7 +343,7 @@
     for row0 in range(0, atoms, CHUNK):
         cut, _, bell, up, down = geometry(own, cols, row0, is_self, basis_count)
         for k, value in enumerate(radial_powers(cut * cut * bell, up, down, basis_count)):
-            store[k, row0 : row0 + CHUNK, :] = value.astype(bf16)
+            store[row0 : row0 + CHUNK, k * atoms : (k + 1) * atoms] = value.astype(bf16)
 
 
 def pick(species_row, table, first):
@@ -128,9 +354,29 @@
     return out
 
 
-def widened(radial, value):
-    return jnp.concatenate(
-        [(radial[k] * value).astype(bf16) for k in range(radial.shape[0])], axis=1
+def split(value):
+    high = value.astype(bf16)
+    return high, (value - high.astype(f32)).astype(bf16)
+
+
+def dot_split(a, value):
+    high, low = split(value)
+    return dot(a, high) + dot(a, low)
+
+
+def widened_split(radial, value):
+    pairs = [split(radial[k] * value) for k in range(radial.shape[0])]
+    return [jnp.concatenate(part, axis=1) for part in zip(*pairs)]
+
+
+def held(value):
+    return value.astype(bf16).astype(f32)
+
+
+def narrowed(radial, sums):
+    atoms = radial.shape[-1]
+    return sum(
+        radial[k] * sums[:, k * atoms : (k + 1) * atoms] for k in range(radial.shape[0])
     )
 
 
@@ -144,19 +390,22 @@
 
 
 def first_kernel(target_of, src, live, pos, send_tab, feat_tab, radial, update_t, send_t,
-                 h1_out, u1_out, s2_out, store):
+                 h1_out, u1_out, s2_out, store, sums):
     basis_count = radial.shape[0]
     channels, atoms = send_tab.shape[1:]
     for b, home in enumerate(target_of):
         own = pos[home]
 
-        def slot(q, total):
+        sums[...] = jnp.zeros_like(sums)
+
+        def slot(q, carry):
             block = pos[src[b, q]]
             fill_kernel(store, own, block.T, q == 0, basis_count)
-            wide = widened(radial, pick(block[3:4, :], send_tab, 1))
-            return total + dot(wide, store[...].reshape(basis_count * atoms, atoms))
-
-        total = lax.fori_loop(0, live[b], slot, jnp.zeros((channels, atoms), f32))
+            sums[...] += dot(pick(block[3:4, :], send_tab, 1).astype(bf16), store[...])
+            return carry
+
+        lax.fori_loop(0, live[b], slot, 0)
+        total = narrowed(radial, sums)
         update = dot(update_t[...], total.astype(bf16))
         species = own[3:4, :]
         hidden = (pick(species, feat_tab, 0) + update * jax.nn.sigmoid(update)).astype(bf16)
@@ -166,37 +415,40 @@
 
 
 def second_kernel(target_of, src, live, pos, s2, h1, radial, update, update_t, out, out_t, energy,
-                  g2_out, dh2_out, ds_out, store, acc):
+                  g2_out, dh2_out, ds_out, store, acc, sums):
     basis_count = radial.shape[0]
     channels, atoms = s2.shape[1:]
     acc[...] = jnp.zeros_like(acc)
     for b, home in enumerate(target_of):
         own = pos[home]
 
-        def gather(q, total):
+        sums[...] = jnp.zeros_like(sums)
+
+        def gather(q, carry):
             where = src[b, q]
             fill_kernel(store.at[q], own, pos[where].T, q == 0, basis_count)
-            wide = widened(radial, s2[where].astype(f32))
-            return total + dot(wide, store[q].reshape(basis_count * atoms, atoms))
-
-        total = lax.fori_loop(0, live[b], gather, jnp.zeros((channels, atoms), f32))
+            sums[...] += dot(s2[where], store[q])
+            return carry
+
+        lax.fori_loop(0, live[b], gather, 0)
+        total = narrowed(radial, sums)
         up = dot(update_t[...], total.astype(bf16))
         second = h1[b].astype(f32) + up * jax.nn.sigmoid(up)
         hidden = dot(out_t[...], second.astype(bf16))
         real = own[3:4, :] > 0.0
         d_hidden = jnp.where(real, energy[...] * silu_grad(hidden), 0.0)
-        d_second = dot(out[...], d_hidden.astype(bf16))
+        d_second = held(dot_split(out[...], d_hidden))
         dh2_out[b] = d_second
-        g2 = dot(update[...], (d_second * silu_grad(up)).astype(bf16)).astype(bf16)
+        g2 = dot_split(update[...], d_second * silu_grad(up)).astype(bf16)
         g2_out[b] = g2
-        wide = widened(radial, g2.astype(f32))
+        wide = jnp.concatenate(widened_split(radial, g2.astype(f32)), axis=0)
 
         def scatter(q, carry):
-            flat = jnp.concatenate([store[q, k] for k in range(basis_count)], axis=1)
             where = src[b, q]
-            acc[where] += lax.dot_general(
-                wide, flat, (((1,), (1,)), ((), ())), preferred_element_type=f32
+            both = lax.dot_general(
+                wide, store[q], (((1,), (1,)), ((), ())), preferred_element_type=f32
             )
+            acc[where] += both[:channels] + both[channels:]
             return carry
 
         lax.fori_loop(0, live[b], scatter, 0)
@@ -220,11 +472,13 @@
     for b, home in enumerate(target_of):
         own = pos[home]
         real = own[3:4, :] > 0.0
-        dh1 = dh2[b] + dot(send[...], ds[b])
+        dh1 = held(dh2[b] + dot(send[...], ds[b]))
         du1 = dh1 * silu_grad(u1[b])
-        g1 = jnp.where(real, dot(update[...], du1.astype(bf16)), 0.0).astype(bf16)
+        g1 = jnp.where(real, dot_split(update[...], du1), 0.0).astype(bf16)
         wide[...] = jnp.concatenate(
-            [widened(radial_one, g1.astype(f32)), widened(radial_two, g2[b].astype(f32))], axis=0
+            widened_split(radial_one, g1.astype(f32))
+            + widened_split(radial_two, g2[b].astype(f32)),
+            axis=0,
         )
         origin = own[:, 0:1]
         own_rel, own_split = split_rows(own - origin)
@@ -233,10 +487,10 @@
             where = src[b, q]
             block = pos[where]
             cols = block.T
-            sender = jnp.concatenate(
-                [pick(block[3:4, :], send_tab, 1), s2[where].astype(f32)], axis=0
-            )
-            parts[...] = dot(sender.T.astype(bf16), wide[...])
+            senders = (pick(block[3:4, :], send_tab, 1), s2[where].astype(f32))
+            turned = [sender.T.astype(bf16) for sender in (senders[0], senders[1])]
+            flipped = jnp.concatenate([turned[0], turned[0], turned[1], turned[1]], axis=1)
+            parts[...] = dot(flipped, wide[...])
             pieces = []
             for row0 in range(0, atoms, CHUNK):
                 cut, inv, bell, up, down = geometry(own, cols, row0, q == 0, basis_count)
@@ -248,13 +502,16 @@
                     moment = moment + centers[k] * term
                 scaled = gamma_width * cut
                 pieces.append(
-                    (cut * (moment * (scaled * inv) - plain * (scaled + 2.0 / cut_sq))).astype(bf16)
+                    (cut * (moment * (scaled * inv) - plain * (scaled + 2.0 / cut_sq)))
                 )
-            slope = jnp.concatenate(pieces, axis=0)
+            high, low = split(jnp.concatenate(pieces, axis=0))
             block_rel, block_split = split_rows(block - origin)
-            at_target = dot(block_split, slope)
-            at_source = lax.dot_general(
-                own_split, slope, (((1,), (1,)), ((), ())), preferred_element_type=f32
+            at_target = dot(block_split, high) + dot(block_split, low)
+            at_source = sum(
+                lax.dot_general(
+                    own_split, part, (((1,), (1,)), ((), ())), preferred_element_type=f32
+                )
+                for part in (high, low)
             )
             at_target = at_target[:8] + at_target[8:]
             at_source = at_source[:8] + at_source[8:]
@@ -306,9 +563,8 @@
     ]
     src, live = slot_tables(neighbour_blocks)
     smem = (src, live)
-    scales = jnp.array(basis_constants(basis_count)[3], f32)
     radial = jnp.broadcast_to(
-        (w_radial * scales[None, :, None])[..., None], (2, basis_count, channels, atoms)
+        w_radial[..., None], (2, basis_count, channels, atoms)
     )
     send_rows = jnp.dot(embedding, w_send[0], preferred_element_type=f32).astype(bf16).astype(f32)
     send_tab = jnp.broadcast_to(send_rows[..., None], (kinds, channels, atoms))
@@ -328,37 +584,41 @@
         return value.reshape((-1,) + value.shape[3:])
 
     def forces(coords):
-        pos = flat(padded(jnp.concatenate([coords, species_row, filler], axis=3)))
+        pos = flat(padded(jnp.concatenate([coords, species_row, filler], axis=3), 0))
         h1, u1, s2_own = call(
             functools.partial(first_kernel, target_of),
             [shaped(blocks, bf16), shaped(blocks, f32), shaped(blocks, bf16)],
-            [pltpu.VMEM((basis_count, atoms, atoms), bf16)],
+            [
+                pltpu.VMEM((atoms, basis_count * atoms), bf16),
+                pltpu.VMEM((channels, basis_count * atoms), f32),
+            ],
             smem,
             (pos, send_tab, feat_tab, radial[0], update_t[0], w_send[1].T),
         )
-        s2 = flat(padded(grid_of(s2_own)))
+        s2 = flat(padded(grid_of(s2_own), 1))
         g2, dh2, ds = call(
             functools.partial(second_kernel, target_of),
             [shaped(blocks, bf16), shaped(blocks, f32), shaped(ext_count, bf16)],
             [
-                pltpu.VMEM((src.shape[1], basis_count, atoms, atoms), bf16),
+                pltpu.VMEM((src.shape[1], atoms, basis_count * atoms), bf16),
                 pltpu.VMEM((ext_count, channels, atoms), f32),
+                pltpu.VMEM((channels, basis_count * atoms), f32),
             ],
             smem,
             (pos, s2, h1, radial[1], w_update[1], update_t[1], w_out, w_out.T, energy),
         )
-        ds_own = flat(folded(ds.reshape(ext_shape + ds.shape[1:])))
+        ds_own = flat(folded(ds.reshape(ext_shape + ds.shape[1:]), 2))
         (grad,) = call(
             functools.partial(third_kernel, target_of),
             [jax.ShapeDtypeStruct((ext_count, 8, atoms), f32)],
             [
-                pltpu.VMEM((2 * channels, basis_count * atoms), bf16),
+                pltpu.VMEM((4 * channels, basis_count * atoms), bf16),
                 pltpu.VMEM((atoms, basis_count * atoms), f32),
             ],
             smem,
             (pos, s2, g2, dh2, ds_own, u1, send_tab, radial[0], radial[1], w_send[1], w_update[0]),
         )
-        total = folded(grad.reshape(ext_shape + grad.shape[1:]))
+        total = folded(grad.reshape(ext_shape + grad.shape[1:]), 3)
         return -total[..., :3, :]
 
     mass = jnp.zeros(species.shape, f32)
@@ -373,13 +633,12 @@
     force_now = forces(coords)
     velocity = half_kick + 0.5 * time_step * force_now * inverse
     real_here = (species > 0).astype(f32)[..., None, :]
-    local_kinetic = jnp.sum(real_here * 0.5 * mass * velocity * velocity)
-    kinetic = lax.psum(local_kinetic, ("gx", "gy", "gz"))
+    part = jnp.sum(real_here * 0.5 * mass * velocity * velocity, axis=(0, 1, 2, 3))
+    part = jnp.broadcast_to(part * 0.125, (8, atoms))
     slot_total = (
         positions.size // 3 * lax.axis_size("gx") * lax.axis_size("gy") * lax.axis_size("gz")
     )
-    factor = jnp.sqrt(target_slot * slot_total / (kinetic + tiny_eps))
-    return (travelled, velocity * factor)
+    return (travelled, thermostat(part, velocity, slot_total, 4))
 
 
 def solution(mesh):

time: 459 us -> 314 us (0.68)
  Pallas kernels: 148 us -> 301 us
  starting transfers between devices: 136 us -> 0 us
  waiting for transfers between devices: 116 us -> 0 us
  blocking collectives: 43 us -> 0 us
    pallas_call x0 -> x9, Pallas kernels: none -> 185 us  [the longest x4 106 us: folded(): pl.pallas_call(fold_kernel, out_shape=jax.ShapeDtypeStruct((x, y, z) + ta...]
    ppermute x48 -> x0, starting transfers between devices: 136 us -> none  [the longest x12 64 us: folded(): from_low = lax.ppermute(high, axis, [(i, i + 1) for i in range(ends)])]
    ppermute x48 -> x0, waiting for transfers between devices: 116 us -> none  [the longest x12 49.9 us: padded(): lax.ppermute(head, axis, [(i + 1, i) for i in range(ends)])]
    psum x1 -> x0, blocking collectives: 43 us -> none  [local(): kinetic = lax.psum(local_kinetic, ('gx', 'gy', 'gz'))]
    pallas_call x6, Pallas kernels: 148 us -> 116 us  [call(): pl.pallas_call(kernel, out_shape=outs, in_specs=[pl.BlockSpec(memory_spac...]
  transfers between devices with their start and end apart: 48 -> 0, of which waited for: 41 -> 0; matrix products, arithmetic and copies ran while one was open for 1% -> 0% of each run, Pallas kernels for 0% -> 0%
where the time goes in v2:
time: 314 us; the launch traced here: 312 us
  Pallas kernels  301 us (96%)
  local copies, waits for them, and re-layouts  6 us (2%)
  other arithmetic  3.54 us (1%)
    pallas_call x6, Pallas kernels, call(): pl.pallas_call(kernel, out_shape=outs, in_specs=[pl.BlockSpec(memory_spac...  116 us
    pallas_call x4, Pallas kernels, folded(): pl.pallas_call(fold_kernel, out_shape=jax.ShapeDtypeStruct((x, y, z) + ta...  106 us
    pallas_call x4, Pallas kernels, padded(): pl.pallas_call(halo_kernel, out_shape=jax.ShapeDtypeStruct(shape, cells.d...  66.1 us
    pallas_call x1, Pallas kernels, thermostat(): pl.pallas_call(functools.partial(thermostat_kernel, float(slot_total)), o...  12.8 us

profile of v2, /device:TPU:0, one launch (start us, length us, event | category | flops | bytes accessed | tf_op | source)
XLA Modules:
  0.0 311.7 jit_solution(1400290715401545553)
XLA Ops:
  0.6 0.8 fusion.11
  1.7 0.5 copy-done.2
  2.3 10.8 %shard_map.122 = f32[4,4,4,8,128]{4,3,2,1,0:T(8,128)S(1)} custom-call(f32[2,2,2,8,128]{4,3,2,1,0:T(8,128)S(1)} %fusion.1.own), custom_call_target="tpu_custom_call" | custom-call | tf_op jit(solution)/shard_map/pallas_call | solution.py:199
  13.1 0.1 broadcast_in_dim.67.radial.radial_one
  13.3 0.6 copy-done.1
  13.9 0.1 copy.14
  14.0 0.7 copy-done.3
  14.7 0.1 fusion
  14.9 0.1 broadcast_in_dim.64.send_tab
  15.0 0.1 copy.15.send_t
  15.1 0.1 broadcast_in_dim.65.feat_tab
  15.2 14.4 %shard_map.123 = (bf16[8,64,128]{2,1,0:T(8,128)(2,1)S(1)}, f32[8,64,128]{2,1,0:T(8,128)S(1)}, bf16[8,64,128]{2,1,0:T(8,128)(2,1)S(1)}) custom-call(s32[8,8]{1,0:T(8,128)S(1)} %bitcast.57, s32[8]{0:T(128)S(1)} %reshape.60.live, f32[64,8,128]{2,1,0:T(8,128)S(1)} %bitcast.45, f32[4,64,128]{2,1,0:T(8,128)S(1)} %broadcast_in_dim.64.send_tab, ...), custom_call_target="tpu_custom_call" | custom-call | tf_op jit(solution)/shard_map/pallas_call | solution.py:526
  29.5 22.5 %shard_map.124 = bf16[4,4,4,64,128]{4,3,2,1,0:T(8,128)(2,1)S(1)} custom-call(bf16[2,2,2,64,128]{4,3,2,1,0:T(8,128)(2,1)S(1)} %bitcast.66), custom_call_target="tpu_custom_call" | custom-call | tf_op jit(solution)/shard_map/pallas_call | solution.py:199
  52.1 0.1 broadcast_in_dim.69.radial.radial_two
  52.2 0.7 copy-done.9
  52.9 0.6 copy-done
  53.7 23.2 %shard_map.125 = (bf16[8,64,128]{2,1,0:T(8,128)(2,1)S(1)}, f32[8,64,128]{2,1,0:T(8,128)S(1)}, bf16[64,64,128]{2,1,0:T(8,128)(2,1)S(1)}) custom-call(s32[8,8]{1,0:T(8,128)S(1)} %bitcast.58, s32[8]{0:T(128)S(1)} %reshape.60.live, f32[64,8,128]{2,1,0:T(8,128)S(1)} %bitcast.46, bf16[64,64,128]{2,1,0:T(8,128)(2,1)S(1)} %bitcast.43, ...), custom_call_target="tpu_custom_call" | custom-call | tf_op jit(solution)/shard_map/pallas_call | solution.py:526
  76.9 28.1 %shard_map.126 = bf16[2,2,2,64,128]{4,3,2,1,0:T(8,128)(2,1)S(1)} custom-call(bf16[4,4,4,64,128]{4,3,2,1,0:T(8,128)(2,1)S(1)} %bitcast.54), custom_call_target="tpu_custom_call" | custom-call | tf_op jit(solution)/shard_map/pallas_call | solution.py:218
  105.0 20.5 %shard_map.127 = f32[64,8,128]{2,1,0:T(8,128)S(1)} custom-call(s32[8,8]{1,0:T(8,128)S(1)} %bitcast.59, s32[8]{0:T(128)S(1)} %reshape.60.live, f32[64,8,128]{2,1,0:T(8,128)S(1)} %bitcast.47, bf16[64,64,128]{2,1,0:T(8,128)(2,1)S(1)} %bitcast.44, bf16[8,64,128]{2,1,0:T(8,128)(2,1)S(1)} %get-tuple-element.16.g2, f32[8,64,128]{2,1,0:T(8,128)S(1)} %get-tuple-element.17.dh2, ...), custom_call_target="tpu_custom_call" | custom-call | tf_op jit(solution)/shard_map/pallas_call | solution.py:526
  125.5 25.1 %shard_map.128 = f32[2,2,2,8,128]{4,3,2,1,0:T(8,128)S(1)} custom-call(f32[4,4,4,8,128]{4,3,2,1,0:T(8,128)S(1)} %bitcast.52), custom_call_target="tpu_custom_call" | custom-call | tf_op jit(solution)/shard_map/pallas_call | solution.py:218
  150.6 0.6 fusion.12
  151.2 2.5 fusion.10
  153.8 9.0 %shard_map.129 = f32[4,4,4,8,128]{4,3,2,1,0:T(8,128)S(1)} custom-call(f32[2,2,2,8,128]{4,3,2,1,0:T(8,128)S(1)} %fusion.2.own), custom_call_target="tpu_custom_call" | custom-call | tf_op jit(solution)/shard_map/pallas_call | solution.py:199
  162.8 14.4 %shard_map.130 = (bf16[8,64,128]{2,1,0:T(8,128)(2,1)S(1)}, f32[8,64,128]{2,1,0:T(8,128)S(1)}, bf16[8,64,128]{2,1,0:T(8,128)(2,1)S(1)}) custom-call(s32[8,8]{1,0:T(8,128)S(1)} %bitcast.60, s32[8]{0:T(128)S(1)} %reshape.60.live, f32[64,8,128]{2,1,0:T(8,128)S(1)} %bitcast.48, f32[4,64,128]{2,1,0:T(8,128)S(1)} %broadcast_in_dim.64.send_tab, ...), custom_call_target="tpu_custom_call" | custom-call | tf_op jit(solution)/shard_map/pallas_call | solution.py:526
  177.2 23.8 %shard_map.131 = bf16[4,4,4,64,128]{4,3,2,1,0:T(8,128)(2,1)S(1)} custom-call(bf16[2,2,2,64,128]{4,3,2,1,0:T(8,128)(2,1)S(1)} %bitcast.65), custom_call_target="tpu_custom_call" | custom-call | tf_op jit(solution)/shard_map/pallas_call | solution.py:199
  201.0 23.2 %shard_map.132 = (bf16[8,64,128]{2,1,0:T(8,128)(2,1)S(1)}, f32[8,64,128]{2,1,0:T(8,128)S(1)}, bf16[64,64,128]{2,1,0:T(8,128)(2,1)S(1)}) custom-call(s32[8,8]{1,0:T(8,128)S(1)} %bitcast.61, s32[8]{0:T(128)S(1)} %reshape.60.live, f32[64,8,128]{2,1,0:T(8,128)S(1)} %bitcast.49, bf16[64,64,128]{2,1,0:T(8,128)(2,1)S(1)} %bitcast.41, ...), custom_call_target="tpu_custom_call" | custom-call | tf_op jit(solution)/shard_map/pallas_call | solution.py:526
  224.2 28.1 %shard_map.133 = bf16[2,2,2,64,128]{4,3,2,1,0:T(8,128)(2,1)S(1)} custom-call(bf16[4,4,4,64,128]{4,3,2,1,0:T(8,128)(2,1)S(1)} %bitcast.53), custom_call_target="tpu_custom_call" | custom-call | tf_op jit(solution)/shard_map/pallas_call | solution.py:218
  252.3 20.3 %shard_map.134 = f32[64,8,128]{2,1,0:T(8,128)S(1)} custom-call(s32[8,8]{1,0:T(8,128)S(1)} %bitcast.62, s32[8]{0:T(128)S(1)} %reshape.60.live, f32[64,8,128]{2,1,0:T(8,128)S(1)} %bitcast.50, bf16[64,64,128]{2,1,0:T(8,128)(2,1)S(1)} %bitcast.42, bf16[8,64,128]{2,1,0:T(8,128)(2,1)S(1)} %get-tuple-element.22.g2, f32[8,64,128]{2,1,0:T(8,128)S(1)} %get-tuple-element.23.dh2, ...), custom_call_target="tpu_custom_call" | custom-call | tf_op jit(solution)/shard_map/pallas_call | solution.py:526
  272.6 25.1 %shard_map.135 = f32[2,2,2,8,128]{4,3,2,1,0:T(8,128)S(1)} custom-call(f32[4,4,4,8,128]{4,3,2,1,0:T(8,128)S(1)} %bitcast.51), custom_call_target="tpu_custom_call" | custom-call | tf_op jit(solution)/shard_map/pallas_call | solution.py:218
  297.7 12.8 %shard_map.136 = f32[2,2,2,3,128]{4,3,2,1,0:T(4,128)S(1)} custom-call(f32[8,128]{1,0:T(8,128)S(1)} %broadcast_in_dim.76.part, f32[2,2,2,3,128]{4,3,2,1,0:T(4,128)S(1)} %get-tuple-element.29.velocity), custom_call_target="tpu_custom_call" | custom-call | tf_op jit(solution)/shard_map/pallas_call | solution.py:275
  310.5 0.6 copy.21
  311.1 0.6 copy.20
  (31 shorter events, 0.6 us)
Async XLA Ops:
  0.6 0.9 copy-start.4
  1.5 0.7 copy-start.2
  2.3 10.8 %copy-start.6 = (f32[2,8,64]{2,1,0:T(8,128)S(1)}, f32[2,8,64]{2,1,0:T(8,128)}, u32[]{:S(2)}) copy-start(f32[2,8,64]{2,1,0:T(8,128)} %param.17) | copy-start | bytes 12292
  13.1 0.8 copy-start.1
  14.0 0.8 copy-start.3
  14.0 0.7 copy-start.8
  52.2 0.7 copy-start.9
  52.9 0.7 copy-start
  125.5 25.1 %copy-start.7 = (f32[4]{0:T(128)S(1)}, f32[4]{0:T(128)}, u32[]{:S(2)}) copy-start(f32[4]{0:T(128)} %param.21) | copy-start | bytes 52
  151.2 2.5 copy-start.5
